TPU v7x, 32 devices: a whole 2x2x4 slice. The times are simulated.
32 devices in a mesh: seq: 2 (over x), fsdp: 2 (over y), ctx: 8 (over z, core).
Axes of the slice: x: 2, y: 2, z: 4, core: 2. Of those that a mesh axis runs over, the one named last changes fastest.
Arguments:
- tokens: bfloat16 [4, 1024, 960], P(('seq', 'fsdp'), 'ctx'), may hold values from -6 to 6
- cotangent: bfloat16 [4, 1024, 960], P(('seq', 'fsdp'), 'ctx'), may hold values from -6 to 6
- block_order: int32 [16], replicated, may hold values from 0 to 15, each once
- gain_attn: float32 [960], replicated, may hold values from 0.5 to 1.5
- gain_mlp: float32 [960], replicated, may hold values from 0.5 to 1.5
- w_query: bfloat16 [960, 960], P(('seq', 'fsdp'), 'ctx'), may hold values from -0.1875 to 0.1875
- w_key: bfloat16 [960, 320], P(('seq', 'fsdp'), 'ctx'), may hold values from -0.1875 to 0.1875
- w_value: bfloat16 [960, 320], P(('seq', 'fsdp'), 'ctx'), may hold values from -0.1875 to 0.1875
- w_out: bfloat16 [960, 960], P(('seq', 'fsdp'), 'ctx'), may hold values from -3 to 3
- w_gate: bfloat16 [960, 2560], P(('seq', 'fsdp'), 'ctx'), may hold values from -0.1875 to 0.1875
- w_up: bfloat16 [960, 2560], P(('seq', 'fsdp'), 'ctx'), may hold values from -0.1875 to 0.1875
- w_down: bfloat16 [2560, 960], P(('seq', 'fsdp'), 'ctx'), may hold values from -0.125 to 0.125
Outputs:
- output: bfloat16 [4, 1024, 960], P(('seq', 'fsdp'), 'ctx')
- input_grad: bfloat16 [4, 1024, 960], P(('seq', 'fsdp'), 'ctx')
- gain_attn_grad: float32 [960], replicated
- gain_mlp_grad: float32 [960], replicated
- query_grad: float32 [960, 960], P(('seq', 'fsdp'), 'ctx')
- key_grad: float32 [960, 320], P(('seq', 'fsdp'), 'ctx')
- value_grad: float32 [960, 320], P(('seq', 'fsdp'), 'ctx')
- out_grad: float32 [960, 960], P(('seq', 'fsdp'), 'ctx')
- gate_grad: float32 [960, 2560], P(('seq', 'fsdp'), 'ctx')
- up_grad: float32 [960, 2560], P(('seq', 'fsdp'), 'ctx')
- down_grad: float32 [2560, 960], P(('seq', 'fsdp'), 'ctx')
Inputs may be any that keep to these rules, and one draw needn't show every extreme that they name: block_order names each block number of one sequence once.
All inputs are finite; a program needn't handle non-finite values.
Results may differ from a plain program's by a relative error of at most 0.023.
Values may be sent and summed in bfloat16 or wider, within the bound.
A program may use at most 128 MiB of HBM per device.

v0:
```python
import math

import jax
import jax.numpy as jnp
from jax import lax
from jax.sharding import PartitionSpec as P

HEADS = 15
KV_HEADS = 5
HEAD_DIM = 64


rope_base = 100000.0
norm_eps = 1e-05


def rope_tables(positions, half_dim):
    freq_index = jnp.arange(half_dim, dtype=jnp.float32)
    inverse = rope_base ** (-freq_index / half_dim)
    angles = positions.astype(jnp.float32)[:, None] * inverse[None, :]
    return (jnp.cos(angles), jnp.sin(angles))


def rotate(values, cosine, sine):
    half_dim = values.shape[-1] // 2
    first_half = values[..., :half_dim]
    second_half = values[..., half_dim:]
    cos_part = cosine[:, None, :]
    sin_part = sine[:, None, :]
    return jnp.concatenate(
        [
            first_half * cos_part - second_half * sin_part,
            second_half * cos_part + first_half * sin_part,
        ],
        axis=-1,
    )


def rotate_back(grads, cosine, sine):
    half_dim = grads.shape[-1] // 2
    first_half = grads[..., :half_dim]
    second_half = grads[..., half_dim:]
    cos_part = cosine[:, None, :]
    sin_part = sine[:, None, :]
    return jnp.concatenate(
        [
            first_half * cos_part + second_half * sin_part,
            second_half * cos_part - first_half * sin_part,
        ],
        axis=-1,
    )


def norm_forward(values, gain):
    inverse_rms = lax.rsqrt(jnp.mean(values * values, axis=1, keepdims=True) + norm_eps)
    scaled = values * inverse_rms
    return (inverse_rms, scaled, (scaled * gain).astype(jnp.bfloat16))


def norm_backward(grad_in, inverse_rms, scaled, gain):
    weighted = grad_in * gain
    back = inverse_rms * (weighted - scaled * jnp.mean(weighted * scaled, axis=1, keepdims=True))
    return (back, jnp.sum(grad_in * scaled, axis=0))


def dot_plain(left, right):
    return jnp.dot(left, right, preferred_element_type=jnp.float32)


def dot_right_trans(left, right):
    return lax.dot_general(
        left, right, (((1,), (1,)), ((), ())), preferred_element_type=jnp.float32
    )


def dot_left_trans(left, right):
    return lax.dot_general(
        left, right, (((0,), (0,)), ((), ())), preferred_element_type=jnp.float32
    )


def on_device(
    tokens,
    cotangent,
    block_order,
    gain_attn,
    gain_mlp,
    w_query,
    w_key,
    w_value,
    w_out,
    w_gate,
    w_up,
    w_down,
):
    row_count = tokens.shape[1]
    block_len = row_count // 2
    ctx_size = lax.axis_size("ctx")
    seq_len = row_count * ctx_size
    block_total = block_order.shape[0]
    group_size = HEADS // KV_HEADS
    kv_width = KV_HEADS * HEAD_DIM
    q_width = HEADS * HEAD_DIM
    scale = 1.0 / math.sqrt(HEAD_DIM)
    slot_index = jnp.arange(seq_len, dtype=jnp.int32)
    owner_hit = (slot_index // block_len)[:, None] == jnp.arange(block_total, dtype=jnp.int32)[
        None, :
    ]
    all_pos = (
        jnp.sum(jnp.where(owner_hit, block_order[None, :], 0), axis=1) * block_len
        + slot_index % block_len
    )
    own_pos = lax.dynamic_slice_in_dim(all_pos, lax.axis_index("ctx") * row_count, row_count)
    cosine, sine = rope_tables(own_pos, HEAD_DIM // 2)
    col_query, col_key, col_value, col_out, col_gate, col_up, col_down = (
        lax.all_gather(w_query, "ctx", axis=1, tiled=True),
        lax.all_gather(w_key, "ctx", axis=1, tiled=True),
        lax.all_gather(w_value, "ctx", axis=1, tiled=True),
        lax.all_gather(w_out, "ctx", axis=1, tiled=True),
        lax.all_gather(w_gate, "ctx", axis=1, tiled=True),
        lax.all_gather(w_up, "ctx", axis=1, tiled=True),
        lax.all_gather(w_down, "ctx", axis=1, tiled=True),
    )
    full_query, full_key, full_value, full_out, full_gate, full_up, full_down = (
        lax.all_gather(col_query, ("seq", "fsdp"), axis=0, tiled=True),
        lax.all_gather(col_key, ("seq", "fsdp"), axis=0, tiled=True),
        lax.all_gather(col_value, ("seq", "fsdp"), axis=0, tiled=True),
        lax.all_gather(col_out, ("seq", "fsdp"), axis=0, tiled=True),
        lax.all_gather(col_gate, ("seq", "fsdp"), axis=0, tiled=True),
        lax.all_gather(col_up, ("seq", "fsdp"), axis=0, tiled=True),
        lax.all_gather(col_down, ("seq", "fsdp"), axis=0, tiled=True),
    )
    token_rows = tokens[0]
    token_f32 = token_rows.astype(jnp.float32)
    rms_attn, unit_attn, normed_attn = norm_forward(token_f32, gain_attn)
    query_raw = dot_plain(normed_attn, full_query).reshape(row_count, HEADS, HEAD_DIM)
    key_raw = dot_plain(normed_attn, full_key).reshape(row_count, KV_HEADS, HEAD_DIM)
    value_raw = dot_plain(normed_attn, full_value)
    query_rot = rotate(query_raw, cosine, sine).astype(jnp.bfloat16)
    key_rot = rotate(key_raw, cosine, sine).reshape(row_count, kv_width).astype(jnp.bfloat16)
    value_bf = value_raw.astype(jnp.bfloat16)
    key_all, value_all = (
        lax.all_gather(key_rot, "ctx", axis=0, tiled=True),
        lax.all_gather(value_bf, "ctx", axis=0, tiled=True),
    )
    key_block = min(512, seq_len)
    num_blocks = seq_len // key_block
    key_blocks = key_all.reshape(num_blocks, key_block, KV_HEADS, HEAD_DIM)
    value_blocks = value_all.reshape(num_blocks, key_block, KV_HEADS, HEAD_DIM)
    pos_blocks = all_pos.reshape(num_blocks, key_block)
    query_group = query_rot.reshape(row_count, KV_HEADS, group_size, HEAD_DIM)

    def block_scores(key_part, pos_part):
        scores = (
            jnp.einsum("rgjd,kgd->gjrk", query_group, key_part, preferred_element_type=jnp.float32)
            * scale
        )
        causal_mask = pos_part[None, :] <= own_pos[:, None]
        return (scores, causal_mask)

    def sum_step(exp_sum, inputs):
        key_part, pos_part = inputs
        scores, causal_mask = block_scores(key_part, pos_part)
        return (exp_sum + jnp.sum(jnp.where(causal_mask, jnp.exp(scores), 0.0), axis=-1), None)

    exp_sum, unused = lax.scan(
        sum_step,
        jnp.zeros((KV_HEADS, group_size, row_count), jnp.float32),
        (key_blocks, pos_blocks),
    )
    log_total = jnp.log(exp_sum)

    def out_step(out_acc, inputs):
        key_part, value_part, pos_part = inputs
        scores, causal_mask = block_scores(key_part, pos_part)
        prob_bf = jnp.where(causal_mask, jnp.exp(scores - log_total[..., None]), 0.0).astype(
            jnp.bfloat16
        )
        return (
            out_acc
            + jnp.einsum("gjrk,kgd->rgjd", prob_bf, value_part, preferred_element_type=jnp.float32),
            None,
        )

    out_sum, unused = lax.scan(
        out_step,
        jnp.zeros((row_count, KV_HEADS, group_size, HEAD_DIM), jnp.float32),
        (key_blocks, value_blocks, pos_blocks),
    )
    attn_bf = out_sum.reshape(row_count, q_width).astype(jnp.bfloat16)
    middle = token_f32 + dot_plain(attn_bf, full_out)
    rms_mlp, unit_mlp, normed_mlp = norm_forward(middle, gain_mlp)
    gate_pre = dot_plain(normed_mlp, full_gate)
    up_pre = dot_plain(normed_mlp, full_up)
    sigmoid_gate = jax.nn.sigmoid(gate_pre)
    silu_gate = gate_pre * sigmoid_gate
    hidden = (silu_gate * up_pre).astype(jnp.bfloat16)
    result = (middle + dot_plain(hidden, full_down)).astype(jnp.bfloat16)
    cot_rows = cotangent[0]
    hidden_grad = dot_right_trans(cot_rows, full_down)
    down_part = dot_left_trans(hidden, cot_rows)
    gate_back = (
        hidden_grad * up_pre * sigmoid_gate * (1.0 + gate_pre * (1.0 - sigmoid_gate))
    ).astype(jnp.bfloat16)
    up_back = (hidden_grad * silu_gate).astype(jnp.bfloat16)
    normed_mlp_grad = dot_right_trans(gate_back, full_gate) + dot_right_trans(up_back, full_up)
    gate_part = dot_left_trans(normed_mlp, gate_back)
    up_part = dot_left_trans(normed_mlp, up_back)
    mlp_back, gain_mlp_part = norm_backward(normed_mlp_grad, rms_mlp, unit_mlp, gain_mlp)
    middle_grad = cot_rows.astype(jnp.float32) + mlp_back
    middle_grad_b = middle_grad.astype(jnp.bfloat16)
    out_part = dot_left_trans(attn_bf, middle_grad_b)
    attn_back = dot_right_trans(middle_grad_b, full_out).astype(jnp.bfloat16)
    grad_group = attn_back.reshape(row_count, KV_HEADS, group_size, HEAD_DIM)
    out_group = attn_bf.reshape(row_count, KV_HEADS, group_size, HEAD_DIM)
    row_delta = jnp.transpose(
        jnp.sum(grad_group.astype(jnp.float32) * out_group.astype(jnp.float32), axis=-1), (1, 2, 0)
    )

    def back_step(query_acc, inputs):
        key_part, value_part, pos_part = inputs
        scores, causal_mask = block_scores(key_part, pos_part)
        probs_full = jnp.where(causal_mask, jnp.exp(scores - log_total[..., None]), 0.0)
        prod_grad = jnp.einsum(
            "rgjd,kgd->gjrk", grad_group, value_part, preferred_element_type=jnp.float32
        )
        score_grad = (probs_full * (prod_grad - row_delta[..., None]) * scale).astype(jnp.bfloat16)
        query_acc = query_acc + jnp.einsum(
            "gjrk,kgd->rgjd", score_grad, key_part, preferred_element_type=jnp.float32
        )
        key_piece = jnp.einsum(
            "gjrk,rgjd->kgd", score_grad, query_group, preferred_element_type=jnp.float32
        )
        value_piece = jnp.einsum(
            "gjrk,rgjd->kgd",
            probs_full.astype(jnp.bfloat16),
            grad_group,
            preferred_element_type=jnp.float32,
        )
        return (query_acc, (key_piece, value_piece))

    query_acc, (key_pieces, value_pieces) = lax.scan(
        back_step,
        jnp.zeros((row_count, KV_HEADS, group_size, HEAD_DIM), jnp.float32),
        (key_blocks, value_blocks, pos_blocks),
    )
    key_own, value_own = (
        lax.psum_scatter(
            key_pieces.reshape(seq_len, kv_width).astype(jnp.bfloat16),
            "ctx",
            scatter_dimension=0,
            tiled=True,
        ).astype(jnp.float32),
        lax.psum_scatter(
            value_pieces.reshape(seq_len, kv_width).astype(jnp.bfloat16),
            "ctx",
            scatter_dimension=0,
            tiled=True,
        ).astype(jnp.float32),
    )
    query_back = (
        rotate_back(query_acc.reshape(row_count, HEADS, HEAD_DIM), cosine, sine)
        .reshape(row_count, q_width)
        .astype(jnp.bfloat16)
    )
    key_back = (
        rotate_back(key_own.reshape(row_count, KV_HEADS, HEAD_DIM), cosine, sine)
        .reshape(row_count, kv_width)
        .astype(jnp.bfloat16)
    )
    value_back = value_own.astype(jnp.bfloat16)
    normed_attn_grad = (
        dot_right_trans(query_back, full_query)
        + dot_right_trans(key_back, full_key)
        + dot_right_trans(value_back, full_value)
    )
    query_part = dot_left_trans(normed_attn, query_back)
    key_part_w = dot_left_trans(normed_attn, key_back)
    value_part_w = dot_left_trans(normed_attn, value_back)
    attn_norm_back, gain_attn_part = norm_backward(normed_attn_grad, rms_attn, unit_attn, gain_attn)
    input_back = (middle_grad + attn_norm_back).astype(jnp.bfloat16)
    gain_attn_sum, gain_mlp_sum = lax.psum((gain_attn_part, gain_mlp_part), ("seq", "fsdp", "ctx"))
    mid_query, mid_key, mid_value, mid_out, mid_gate, mid_up, mid_down = (
        lax.psum_scatter(
            query_part.astype(jnp.bfloat16), "ctx", scatter_dimension=1, tiled=True
        ).astype(jnp.float32),
        lax.psum_scatter(
            key_part_w.astype(jnp.bfloat16), "ctx", scatter_dimension=1, tiled=True
        ).astype(jnp.float32),
        lax.psum_scatter(
            value_part_w.astype(jnp.bfloat16), "ctx", scatter_dimension=1, tiled=True
        ).astype(jnp.float32),
        lax.psum_scatter(
            out_part.astype(jnp.bfloat16), "ctx", scatter_dimension=1, tiled=True
        ).astype(jnp.float32),
        lax.psum_scatter(
            gate_part.astype(jnp.bfloat16), "ctx", scatter_dimension=1, tiled=True
        ).astype(jnp.float32),
        lax.psum_scatter(
            up_part.astype(jnp.bfloat16), "ctx", scatter_dimension=1, tiled=True
        ).astype(jnp.float32),
        lax.psum_scatter(
            down_part.astype(jnp.bfloat16), "ctx", scatter_dimension=1, tiled=True
        ).astype(jnp.float32),
    )
    fin_query, fin_key, fin_value, fin_out, fin_gate, fin_up, fin_down = (
        lax.psum_scatter(
            mid_query.astype(jnp.bfloat16), ("seq", "fsdp"), scatter_dimension=0, tiled=True
        ).astype(jnp.float32),
        lax.psum_scatter(
            mid_key.astype(jnp.bfloat16), ("seq", "fsdp"), scatter_dimension=0, tiled=True
        ).astype(jnp.float32),
        lax.psum_scatter(
            mid_value.astype(jnp.bfloat16), ("seq", "fsdp"), scatter_dimension=0, tiled=True
        ).astype(jnp.float32),
        lax.psum_scatter(
            mid_out.astype(jnp.bfloat16), ("seq", "fsdp"), scatter_dimension=0, tiled=True
        ).astype(jnp.float32),
        lax.psum_scatter(
            mid_gate.astype(jnp.bfloat16), ("seq", "fsdp"), scatter_dimension=0, tiled=True
        ).astype(jnp.float32),
        lax.psum_scatter(
            mid_up.astype(jnp.bfloat16), ("seq", "fsdp"), scatter_dimension=0, tiled=True
        ).astype(jnp.float32),
        lax.psum_scatter(
            mid_down.astype(jnp.bfloat16), ("seq", "fsdp"), scatter_dimension=0, tiled=True
        ).astype(jnp.float32),
    )
    return (
        result.reshape(1, row_count, result.shape[1]),
        input_back.reshape(1, row_count, input_back.shape[1]),
        gain_attn_sum,
        gain_mlp_sum,
        fin_query,
        fin_key,
        fin_value,
        fin_out,
        fin_gate,
        fin_up,
        fin_down,
    )


def solution(mesh):
    return jax.shard_map(
        on_device,
        mesh=mesh,
        in_specs=(
            P(("seq", "fsdp"), "ctx", None),
            P(("seq", "fsdp"), "ctx", None),
            P(),
            P(),
            P(),
            P(("seq", "fsdp"), "ctx"),
            P(("seq", "fsdp"), "ctx"),
            P(("seq", "fsdp"), "ctx"),
            P(("seq", "fsdp"), "ctx"),
            P(("seq", "fsdp"), "ctx"),
            P(("seq", "fsdp"), "ctx"),
            P(("seq", "fsdp"), "ctx"),
        ),
        out_specs=(
            P(("seq", "fsdp"), "ctx", None),
            P(("seq", "fsdp"), "ctx", None),
            P(),
            P(),
            P(("seq", "fsdp"), "ctx"),
            P(("seq", "fsdp"), "ctx"),
            P(("seq", "fsdp"), "ctx"),
            P(("seq", "fsdp"), "ctx"),
            P(("seq", "fsdp"), "ctx"),
            P(("seq", "fsdp"), "ctx"),
            P(("seq", "fsdp"), "ctx"),
        ),
        check_vma=False,
    )
```

profile of v0, /device:TPU:0, one launch (start us, length us, event | category | flops | bytes accessed | tf_op | source)
XLA Modules:
  0.0 908.9 jit_solution(7911319518605280512)
XLA Ops:
  10.4 17.4 %all_gather.54 = bf16[240,960]{0,1:T(8,128)(2,1)S(1)} all-gather(bf16[240,120]{0,1:T(8,128)(2,1)S(1)} %copy.88), channel_id=1, replica_groups=mesh['seq'=2,'fsdp'=2,'ctx'=8] {'ctx'}, dimensions={1}, use_global_device_ids=true | all-gather | bytes 518400 | tf_op jit(solution)/shard_map/all_gather | solution.py:116
  29.8 15.1 %all_gather.56 = bf16[240,960]{0,1:T(8,128)(2,1)S(1)} all-gather(bf16[240,120]{0,1:T(8,128)(2,1)S(1)} %copy.94), channel_id=1, replica_groups=mesh['seq'=2,'fsdp'=2,'ctx'=8] {'ctx'}, dimensions={1}, use_global_device_ids=true | all-gather | bytes 518400 | tf_op jit(solution)/shard_map/all_gather | solution.py:119
  48.6 13.3 %all-gather.19.cloned.1.call-done = bf16[240,2560]{0,1:T(8,128)(2,1)} async-done(((bf16[240,320]{0,1:T(8,128)(2,1)}), bf16[240,2560]{0,1:T(8,128)(2,1)}) %all-gather.19.cloned.1.call-update) | async-done | bytes 1228816 | tf_op jit(solution)/shard_map/all_gather | solution.py:121
  64.5 14.6 %all_gather.48 = bf16[240,320]{0,1:T(8,128)(2,1)S(1)} all-gather(bf16[240,40]{0,1:T(8,128)(2,1)S(1)} %copy-done.34), channel_id=1, replica_groups=mesh['seq'=2,'fsdp'=2,'ctx'=8] {'ctx'}, dimensions={1}, use_global_device_ids=true | all-gather | bytes 172800 | tf_op jit(solution)/shard_map/all_gather | solution.py:118
  79.1 11.4 %all-gather = bf16[4,240,320]{1,2,0:T(8,128)(2,1)S(1)} all-gather(bf16[1,240,320]{1,2,0:T(8,128)(2,1)S(1)} %bitcast.323), channel_id=1, replica_groups=mesh['seq'=2,'fsdp'=2,'ctx'=8] {'seq','fsdp'}, dimensions={0}, use_global_device_ids=true | all-gather | bytes 768000 | tf_op jit(solution)/shard_map/all_gather | solution.py:127
  92.3 14.5 %all_gather.50 = bf16[1024,320]{0,1:T(8,128)(2,1)S(1)} all-gather(bf16[128,320]{0,1:T(8,128)(2,1)S(1)} %convolution_convert_fusion.8), channel_id=1, replica_groups=mesh['seq'=2,'fsdp'=2,'ctx'=8] {'ctx'}, dimensions={0}, use_global_device_ids=true | all-gather | bytes 737280 | tf_op jit(solution)/shard_map/all_gather | solution.py:144
  108.4 14.0 %all_gather.51 = bf16[240,320]{0,1:T(8,128)(2,1)S(1)} all-gather(bf16[240,40]{0,1:T(8,128)(2,1)S(1)} %copy-done.35), channel_id=1, replica_groups=mesh['seq'=2,'fsdp'=2,'ctx'=8] {'ctx'}, dimensions={1}, use_global_device_ids=true | all-gather | bytes 172800 | tf_op jit(solution)/shard_map/all_gather | solution.py:117
  122.5 11.5 %all-gather.1 = bf16[4,240,320]{1,2,0:T(8,128)(2,1)S(1)} all-gather(bf16[1,240,320]{1,2,0:T(8,128)(2,1)S(1)} %bitcast.324), channel_id=1, replica_groups=mesh['seq'=2,'fsdp'=2,'ctx'=8] {'seq','fsdp'}, dimensions={0}, use_global_device_ids=true | all-gather | bytes 768000 | tf_op jit(solution)/shard_map/all_gather | solution.py:126
  135.8 14.7 %all_gather.53 = bf16[1024,320]{0,1:T(8,128)(2,1)S(1)} all-gather(bf16[128,320]{0,1:T(8,128)(2,1)S(1)} %bitcast.328), channel_id=1, replica_groups=mesh['seq'=2,'fsdp'=2,'ctx'=8] {'ctx'}, dimensions={0}, use_global_device_ids=true | all-gather | bytes 737280 | tf_op jit(solution)/shard_map/all_gather | solution.py:143
  162.9 54.9 %all-gather.17.cloned.1.call-done = bf16[960,2560]{1,0:T(8,128)(2,1)} async-done(((bf16[240,2560]{1,0:T(8,128)(2,1)}), bf16[960,2560]{1,0:T(8,128)(2,1)}) %all-gather.17.cloned.1.call-update) | async-done | bytes 4915216 | tf_op jit(solution)/shard_map/all_gather | solution.py:129
  217.8 4.3 fusion.98
  222.2 56.1 %all-gather.21.cloned.1.call-done = bf16[960,2560]{1,0:T(8,128)(2,1)} async-done(((bf16[240,2560]{1,0:T(8,128)(2,1)}), bf16[960,2560]{1,0:T(8,128)(2,1)}) %all-gather.21.cloned.1.call-update) | async-done | bytes 4915216 | tf_op jit(solution)/shard_map/all_gather | solution.py:130
  278.3 4.3 fusion.99
  282.6 56.1 %all-gather.25.cloned.1.call-done = bf16[2560,960]{0,1:T(8,128)(2,1)} async-done(((bf16[640,960]{0,1:T(8,128)(2,1)}), bf16[2560,960]{0,1:T(8,128)(2,1)}) %all-gather.25.cloned.1.call-update) | async-done | bytes 4915216 | tf_op jit(solution)/shard_map/all_gather | solution.py:131
  338.7 5.3 multiply_convert_fusion
  344.1 4.3 fusion.100
  351.2 20.3 %while.39 = (s32[]{:T(128)}, f32[128,5,3,64]{0,3,2,1:T(8,128)}, bf16[2,512,5,64]{1,3,2,0:T(8,128)(2,1)}, bf16[2,512,5,64]{1,3,2,0:T(8,128)(2,1)}, bf16[2,512,5,6...) while((s32[]{:T(128)}, f32[128,5,3,64]{0,3,2,1:T(8,128)}, ...), condition=%wide.region_11.12_spmd.clone, body=%wide.region_10.11_spmd.clone.sunk | while | flops 640270336 | bytes 63476592 | solution.py:242
  383.4 4.8 convolution_convert_fusion.2
  388.3 18.4 %reduce-scatter.41.cloned.1.call-done = bf16[128,320]{1,0:T(8,128)(2,1)} async-done(((bf16[1024,320]{1,0:T(8,128)(2,1)}), bf16[128,320]{1,0:T(8,128)(2,1)}) %reduce-scatter.41.cloned.1.call-update) | async-done | bytes 81936
  409.1 30.0 %reduce-scatter.43.cloned.1.call-done = bf16[128,320]{1,0:T(8,128)(2,1)} async-done(((bf16[1024,320]{1,0:T(8,128)(2,1)}), bf16[128,320]{1,0:T(8,128)(2,1)}) %reduce-scatter.43.cloned.1.call-update) | async-done | bytes 81936
  450.5 25.1 %reduce-scatter.45.cloned.1.call-done = bf16[120,960]{1,0:T(8,128)(2,1)} async-done(((bf16[960,960]{1,0:T(8,128)(2,1)}), bf16[120,960]{1,0:T(8,128)(2,1)}) %reduce-scatter.45.cloned.1.call-update) | async-done | bytes 230416
  477.4 34.4 %reduce-scatter.47.cloned.1.call-done = bf16[120,960]{1,0:T(8,128)(2,1)} async-done(((bf16[960,960]{1,0:T(8,128)(2,1)}), bf16[120,960]{1,0:T(8,128)(2,1)}) %reduce-scatter.47.cloned.1.call-update) | async-done | bytes 230416
  513.7 55.4 %reduce-scatter.39.cloned.1.call-done = bf16[2560,120]{0,1:T(8,128)(2,1)} async-done(((bf16[2560,960]{0,1:T(8,128)(2,1)}), bf16[2560,120]{0,1:T(8,128)(2,1)}) %reduce-scatter.39.cloned.1.call-update) | async-done | bytes 614416 | tf_op jit(solution)/shard_map/reduce_scatter | solution.py:302
  572.6 28.7 %reduce-scatter.31.cloned.1.call-done = bf16[960,40]{0,1:T(8,128)(2,1)} async-done(((bf16[960,320]{0,1:T(8,128)(2,1)}), bf16[960,40]{0,1:T(8,128)(2,1)}) %reduce-scatter.31.cloned.1.call-update) | async-done | bytes 76816 | tf_op jit(solution)/shard_map/reduce_scatter | solution.py:287
  601.3 32.0 %reduce-scatter.33.cloned.1.call-done = bf16[960,40]{0,1:T(8,128)(2,1)} async-done(((bf16[960,320]{0,1:T(8,128)(2,1)}), bf16[960,40]{0,1:T(8,128)(2,1)}) %reduce-scatter.33.cloned.1.call-update) | async-done | bytes 76816 | tf_op jit(solution)/shard_map/reduce_scatter | solution.py:290
  633.3 60.3 %reduce-scatter.35.cloned.1.call-done = bf16[960,320]{0,1:T(8,128)(2,1)} async-done(((bf16[960,2560]{0,1:T(8,128)(2,1)}), bf16[960,320]{0,1:T(8,128)(2,1)}) %reduce-scatter.35.cloned.1.call-update) | async-done | bytes 614416 | tf_op jit(solution)/shard_map/reduce_scatter | solution.py:296
  693.6 60.5 %reduce-scatter.37.cloned.1.call-done = bf16[960,320]{0,1:T(8,128)(2,1)} async-done(((bf16[960,2560]{0,1:T(8,128)(2,1)}), bf16[960,320]{0,1:T(8,128)(2,1)}) %reduce-scatter.37.cloned.1.call-update) | async-done | bytes 614416 | tf_op jit(solution)/shard_map/reduce_scatter | solution.py:299
  754.1 4.7 fusion.52
  760.6 37.9 %all-reduce.6 = (f32[960]{0:T(1024)}, f32[960]{0:T(1024)}) all-reduce(f32[960]{0:T(1024)S(1)} %get-tuple-element.367, f32[960]{0:T(1024)S(1)} %get-tuple-element.365), channel_id=1, replica_groups=mesh['seq'=2,'fsdp'=2,'ctx'=8] {'seq','fsdp','ctx'}, use_global_device_ids=true, to_apply=%region_16.17 | all-reduce | flops 1920 | bytes 15360 | tf_op jit(solution)/shard_map/psum | solution.py:282
  800.8 5.9 reduce-scatter.53.cloned.1.call-done
  808.3 26.9 %reduce-scatter.49.cloned.1.call-done = bf16[640,120]{1,0:T(8,128)(2,1)} async-done(((bf16[2560,120]{1,0:T(8,128)(2,1)}), bf16[640,120]{1,0:T(8,128)(2,1)}) %reduce-scatter.49.cloned.1.call-update) | async-done | bytes 153616
  837.0 61.1 %all-reduce.10.cloned.1.call-done = (bf16[960,40]{0,1:T(8,128)(2,1)}, bf16[960,40]{0,1:T(8,128)(2,1)}, bf16[960,320]{0,1:T(8,128)(2,1)}, bf16[960,320]{0,1:T(8,128)(2,1)}) async-done(((bf16[960,40]{0,1:T(8,128)(2,1)}, bf16[960,40]{0,1:T(8,128)(2,1)}, bf16[960,320]{0,1:T(8,128)(2,1)}, bf16[960,320]{0,1:T(8,128)(2,1)}), (bf16[960,40]{0,1:T(8,128)(2,1)}, bf16[960,40]{0,1:T(8,128)(2,1)}, ...) | async-done | bytes 1382416
  (249 shorter events, 99.2 us)
Async XLA Ops:
  7.2 38.9 %all-gather.15.cloned.1.call-start = ((), (), s32[]{:S(2)}) async-start(), calls=%async_computation.14 | async-start | bytes 1474560 | tf_op jit(solution)/shard_map/all_gather | solution.py:120
  7.9 54.1 %all-gather.19.cloned.1.call-start = ((), (), s32[]{:S(2)}) async-start(), calls=%async_computation.16 | async-start | bytes 1474560 | tf_op jit(solution)/shard_map/all_gather | solution.py:121
  8.7 83.6 %all-gather.23.cloned.1.call-start = ((), (), s32[]{:S(2)}) async-start(), calls=%async_computation.18 | async-start | bytes 1382400 | tf_op jit(solution)/shard_map/all_gather | solution.py:122
  9.4 141.6 %all-gather.11.cloned.1.call-start = ((), (), s32[]{:S(2)}) async-start(), calls=%async_computation.12 | async-start | bytes 2457600 | tf_op jit(solution)/shard_map/all_gather | solution.py:125
  28.8 131.3 %all-gather.13.cloned.1.call-start = ((), (), s32[]{:S(2)}) async-start(), calls=%async_computation.13 | async-start | bytes 2457600 | tf_op jit(solution)/shard_map/all_gather | solution.py:128
  45.9 18.5 %copy-start.34 = (bf16[240,40]{0,1:T(8,128)(2,1)S(1)}, bf16[240,40]{0,1:T(8,128)(2,1)}, u32[]{:S(2)}) copy-start(bf16[240,40]{0,1:T(8,128)(2,1)} %param.25) | copy-start | bytes 57604
  46.0 171.9 %all-gather.17.cloned.1.call-start = ((), (), s32[]{:S(2)}) async-start(), calls=%async_computation.15 | async-start | bytes 6144000 | tf_op jit(solution)/shard_map/all_gather | solution.py:129
  48.6 43.0 %copy-start.2 = (bf16[1,128,960]{1,2,0:T(8,128)(2,1)S(1)}, bf16[1,128,960]{1,2,0:T(8,128)(2,1)}, u32[]{:S(2)}) copy-start(bf16[1,128,960]{1,2,0:T(8,128)(2,1)} %param.18) | copy-start | bytes 737284
  48.6 43.2 %copy-start.32 = (f32[960]{0:T(1024)S(1)}, f32[960]{0:T(1024)}, u32[]{:S(2)}) copy-start(f32[960]{0:T(1024)} %param.21) | copy-start | bytes 11524
  48.6 229.7 %all-gather.21.cloned.1.call-start = ((), (), s32[]{:S(2)}) async-start(), calls=%async_computation.17 | async-start | bytes 6144000 | tf_op jit(solution)/shard_map/all_gather | solution.py:130
  64.4 274.3 %all-gather.25.cloned.1.call-start = ((), (), s32[]{:S(2)}) async-start(), calls=%async_computation.19 | async-start | bytes 6144000 | tf_op jit(solution)/shard_map/all_gather | solution.py:131
  91.6 42.3 %copy-start.18 = (bf16[960,320]{0,1:T(8,128)(2,1)}, bf16[960,320]{0,1:T(8,128)(2,1)S(1)}, u32[]{:S(2)}) copy-start(bf16[960,320]{0,1:T(8,128)(2,1)S(1)} %reshape.251) | copy-start | bytes 1843204
  92.3 314.4 %reduce-scatter.41.cloned.1.call-start = ((), (), s32[]{:S(2)}) async-start(), calls=%async_computation.25 | async-start | bytes 884736
  162.7 187.3 %copy-start.5 = (f32[128,960]{0,1:T(8,128)}, f32[128,960]{0,1:T(8,128)S(1)}, u32[]{:S(2)}) copy-start(f32[128,960]{0,1:T(8,128)S(1)} %get-tuple-element.445) | copy-start | bytes 1474564
  222.2 116.6 %copy-start.23 = (bf16[1,128,960]{1,2,0:T(8,128)(2,1)S(1)}, bf16[1,128,960]{1,2,0:T(8,128)(2,1)}, u32[]{:S(2)}) copy-start(bf16[1,128,960]{1,2,0:T(8,128)(2,1)} %param.19) | copy-start | bytes 737284
  374.6 64.5 %reduce-scatter.43.cloned.1.call-start = ((), (), s32[]{:S(2)}) async-start(), calls=%async_computation.26 | async-start | bytes 884736
  376.7 98.9 %reduce-scatter.45.cloned.1.call-start = ((), (), s32[]{:S(2)}) async-start(), calls=%async_computation.27 | async-start | bytes 2211840
  380.1 131.7 %reduce-scatter.47.cloned.1.call-start = ((), (), s32[]{:S(2)}) async-start(), calls=%async_computation.28 | async-start | bytes 2211840
  383.4 185.7 %reduce-scatter.39.cloned.1.call-start = ((), (), s32[]{:S(2)}) async-start(), calls=%async_computation.24 | async-start | bytes 5529600 | tf_op jit(solution)/shard_map/reduce_scatter | solution.py:302
  388.2 53.2 %copy-start.17 = (bf16[128,2560]{1,0:T(8,128)(2,1)S(1)}, bf16[128,2560]{1,0:T(8,128)(2,1)}, u32[]{:S(2)}) copy-start(bf16[128,2560]{1,0:T(8,128)(2,1)} %copy-done.16) | copy-start | bytes 1966084
  388.3 213.1 %reduce-scatter.31.cloned.1.call-start = ((), (), s32[]{:S(2)}) async-start(), calls=%async_computation.20 | async-start | bytes 737280 | tf_op jit(solution)/shard_map/reduce_scatter | solution.py:287
  409.1 224.3 %reduce-scatter.33.cloned.1.call-start = ((), (), s32[]{:S(2)}) async-start(), calls=%async_computation.21 | async-start | bytes 737280 | tf_op jit(solution)/shard_map/reduce_scatter | solution.py:290
  441.3 252.3 %reduce-scatter.35.cloned.1.call-start = ((), (), s32[]{:S(2)}) async-start(), calls=%async_computation.22 | async-start | bytes 5898240 | tf_op jit(solution)/shard_map/reduce_scatter | solution.py:296
  445.3 308.7 %reduce-scatter.37.cloned.1.call-start = ((), (), s32[]{:S(2)}) async-start(), calls=%async_computation.23 | async-start | bytes 5898240 | tf_op jit(solution)/shard_map/reduce_scatter | solution.py:299
  450.4 121.0 %copy-start.37 = (u32[32]{0:T(128)S(1)}, u32[32]{0:T(128)}, u32[]{:S(2)}) copy-start(u32[32]{0:T(128)} %constant.109) | copy-start | bytes 388
  450.4 303.7 %copy-start.6 = (f32[128,960]{0,1:T(8,128)S(1)}, f32[128,960]{0,1:T(8,128)}, u32[]{:S(2)}) copy-start(f32[128,960]{0,1:T(8,128)} %copy-done.5) | copy-start | bytes 1474564
  450.4 303.7 %copy-start.13 = (bf16[128,2560]{1,0:T(8,128)(2,1)S(1)}, bf16[128,2560]{1,0:T(8,128)(2,1)}, u32[]{:S(2)}) copy-start(bf16[128,2560]{1,0:T(8,128)(2,1)} %get-tuple-element.431) | copy-start | bytes 1966084
  450.4 349.0 %reduce-scatter.51.cloned.1.call-start = ((), (), s32[]{:S(2)}) async-start(), calls=%async_computation.30 | async-start | bytes 307200
  477.4 329.4 %reduce-scatter.53.cloned.1.call-start = ((), (), s32[]{:S(2)}) async-start(), calls=%async_computation.31 | async-start | bytes 307200
  513.6 321.6 %reduce-scatter.49.cloned.1.call-start = ((), (), s32[]{:S(2)}) async-start(), calls=%async_computation.29 | async-start | bytes 819200
  571.3 187.5 %copy-start.12 = (bf16[960,320]{0,1:T(8,128)(2,1)S(1)}, bf16[960,320]{0,1:T(8,128)(2,1)}, u32[]{:S(2)}) copy-start(bf16[960,320]{0,1:T(8,128)(2,1)} %copy-done.11) | copy-start | bytes 1843204
  571.3 326.8 %all-reduce.10.cloned.1.call-start = ((), (), s32[]{:S(2)}) async-start(), calls=%async_computation.32 | async-start | bytes 2949120
  (34 other events, 141.6 us)
Sparse Core Ops, SparseCore 0:
  9.6 27.8 all-gather.14
  39.2 22.7 all-gather.18
  63.6 23.0 all-gather.22
  88.4 33.2 all-gather.10
  123.4 34.0 all-gather.12
  159.2 58.5 all-gather.16
  219.7 58.5 all-gather.20
  280.1 58.5 all-gather.24
  374.8 31.8 reduce-scatter.40
  408.8 30.2 reduce-scatter.42
  441.4 34.1 reduce-scatter.44
  477.8 33.9 reduce-scatter.46
  514.1 54.9 reduce-scatter.38
  571.2 30.0 reduce-scatter.30
  603.4 29.8 reduce-scatter.32
  635.5 58.0 reduce-scatter.34
  695.8 58.2 reduce-scatter.36
  757.3 22.2 reduce-scatter.50
  782.9 23.8 reduce-scatter.52
  809.5 25.6 reduce-scatter.48
  838.6 59.3 all-reduce.9
where the time goes:
time: 916 us; the launch traced here: 909 us
  waiting for transfers between devices  622 us (68%)
  blocking collectives  151 us (16%)
  matrix products  70.3 us (8%)
  local copies, waits for them, and re-layouts  37.6 us (4%)
  between operations  16.2 us (2%)
  other arithmetic  10.3 us (1%)
    unnamed x29, waiting for transfers between devices  204 us
    reduce_scatter x1, waiting for transfers between devices, on_device(): lax.psum_scatter(up_part.astype(jnp.bfloat16), 'ctx', scatter_dimension=1...  60.5 us
    reduce_scatter x1, waiting for transfers between devices, on_device(): lax.psum_scatter(gate_part.astype(jnp.bfloat16), 'ctx', scatter_dimension...  60.3 us
    all_gather x1, waiting for transfers between devices, on_device(): lax.all_gather(col_down, ('seq', 'fsdp'), axis=0, tiled=True)  56.1 us
    all_gather x1, waiting for transfers between devices, on_device(): lax.all_gather(col_up, ('seq', 'fsdp'), axis=0, tiled=True)  56.1 us
    reduce_scatter x1, waiting for transfers between devices, on_device(): lax.psum_scatter(down_part.astype(jnp.bfloat16), 'ctx', scatter_dimension...  55.4 us
    all_gather x1, waiting for transfers between devices, on_device(): lax.all_gather(col_gate, ('seq', 'fsdp'), axis=0, tiled=True)  54.9 us
    psum x1, blocking collectives, on_device(): lax.psum((gain_attn_part, gain_mlp_part), ('seq', 'fsdp', 'ctx'))  37.9 us
  transfers between devices with their start and end apart: 21, of which 16 were waited for; matrix products, arithmetic and copies ran while one was open for 9% of the time, Pallas kernels for 0%

commit v1 on v0

v1 whole, which is shorter than its diff:
```python
import math

import jax
import jax.numpy as jnp
from jax import lax
from jax.sharding import PartitionSpec as P

HEADS = 15
KV_HEADS = 5
HEAD_DIM = 64


rope_base = 100000.0
norm_eps = 1e-05


def rope_tables(positions, half_dim):
    freq_index = jnp.arange(half_dim, dtype=jnp.float32)
    inverse = rope_base ** (-freq_index / half_dim)
    angles = positions.astype(jnp.float32)[:, None] * inverse[None, :]
    return (jnp.cos(angles), jnp.sin(angles))


def rotate(values, cosine, sine):
    half_dim = values.shape[-1] // 2
    first_half = values[..., :half_dim]
    second_half = values[..., half_dim:]
    cos_part = cosine[:, None, :]
    sin_part = sine[:, None, :]
    return jnp.concatenate(
        [
            first_half * cos_part - second_half * sin_part,
            second_half * cos_part + first_half * sin_part,
        ],
        axis=-1,
    )


def rotate_back(grads, cosine, sine):
    half_dim = grads.shape[-1] // 2
    first_half = grads[..., :half_dim]
    second_half = grads[..., half_dim:]
    cos_part = cosine[:, None, :]
    sin_part = sine[:, None, :]
    return jnp.concatenate(
        [
            first_half * cos_part + second_half * sin_part,
            second_half * cos_part - first_half * sin_part,
        ],
        axis=-1,
    )


def norm_forward(values, gain):
    inverse_rms = lax.rsqrt(jnp.mean(values * values, axis=1, keepdims=True) + norm_eps)
    scaled = values * inverse_rms
    return (inverse_rms, scaled, (scaled * gain).astype(jnp.bfloat16))


def norm_backward(grad_in, inverse_rms, scaled, gain):
    weighted = grad_in * gain
    back = inverse_rms * (weighted - scaled * jnp.mean(weighted * scaled, axis=1, keepdims=True))
    return (back, jnp.sum(grad_in * scaled, axis=0))


def dot_plain(left, right):
    return jnp.dot(left, right, preferred_element_type=jnp.float32)


def dot_right_trans(left, right):
    return lax.dot_general(
        left, right, (((1,), (1,)), ((), ())), preferred_element_type=jnp.float32
    )


def dot_left_trans(left, right):
    return lax.dot_general(
        left, right, (((0,), (0,)), ((), ())), preferred_element_type=jnp.float32
    )


def on_device(
    tokens,
    cotangent,
    block_order,
    gain_attn,
    gain_mlp,
    w_query,
    w_key,
    w_value,
    w_out,
    w_gate,
    w_up,
    w_down,
):
    rows_axes = ("seq", "fsdp")
    bf16 = jnp.bfloat16
    row_count, width = tokens.shape[1], tokens.shape[2]
    ctx_size = lax.axis_size("ctx")
    seq_len = row_count * ctx_size
    block_total = block_order.shape[0]
    block_len = seq_len // block_total
    group_size = HEADS // KV_HEADS
    kv_width = KV_HEADS * HEAD_DIM
    q_width = HEADS * HEAD_DIM
    q_cols, kv_cols, ff_cols = w_query.shape[1], w_key.shape[1], w_gate.shape[1]
    qkv_cols = q_cols + 2 * kv_cols
    attn_cols = qkv_cols + w_out.shape[1]
    scale = 1.0 / math.sqrt(HEAD_DIM)
    slot_index = jnp.arange(seq_len, dtype=jnp.int32)
    owner_hit = (slot_index // block_len)[:, None] == jnp.arange(block_total, dtype=jnp.int32)[
        None, :
    ]
    all_pos = (
        jnp.sum(jnp.where(owner_hit, block_order[None, :], 0), axis=1) * block_len
        + slot_index % block_len
    )
    own_pos = lax.dynamic_slice_in_dim(all_pos, lax.axis_index("ctx") * row_count, row_count)
    cosine, sine = rope_tables(own_pos, HEAD_DIM // 2)
    row_parts = lax.axis_size(rows_axes)

    def scatter_rows(part):
        pieces = part.reshape(row_parts, part.shape[0] // row_parts, part.shape[1])
        pieces = lax.all_to_all(pieces, rows_axes, split_axis=0, concat_axis=0, tiled=True)
        return jnp.sum(pieces.astype(jnp.float32), axis=0)

    attn_rows = lax.all_gather(
        jnp.concatenate([w_query, w_key, w_value, w_out], axis=1), rows_axes, axis=0, tiled=True
    )
    qkv_full = lax.all_gather(attn_rows[:, :qkv_cols], "ctx", axis=0)
    out_full = lax.all_gather(attn_rows[:, qkv_cols:], "ctx", axis=1, tiled=True)
    gate_up = lax.all_gather(
        jnp.concatenate([w_gate, w_up], axis=1), rows_axes, axis=0, tiled=True
    )
    gate_w, up_w = gate_up[:, :ff_cols], gate_up[:, ff_cols:]
    down_w = lax.all_to_all(
        lax.all_gather(w_down, rows_axes, axis=0, tiled=True),
        "ctx",
        split_axis=0,
        concat_axis=1,
        tiled=True,
    )
    cot_rows = cotangent[0]
    cot_all = lax.all_gather(cot_rows, "ctx", axis=0, tiled=True)

    token_f32 = tokens[0].astype(jnp.float32)
    rms_attn, unit_attn, normed_attn = norm_forward(token_f32, gain_attn)
    qkv = jnp.einsum("td,cdf->tcf", normed_attn, qkv_full, preferred_element_type=jnp.float32)
    query_raw = qkv[:, :, :q_cols].reshape(row_count, HEADS, HEAD_DIM)
    key_raw = qkv[:, :, q_cols : q_cols + kv_cols].reshape(row_count, KV_HEADS, HEAD_DIM)
    value_bf = qkv[:, :, q_cols + kv_cols :].reshape(row_count, kv_width).astype(bf16)
    query_rot = rotate(query_raw, cosine, sine).astype(bf16)
    key_rot = rotate(key_raw, cosine, sine).reshape(row_count, kv_width).astype(bf16)
    kv_all = lax.all_gather(
        jnp.concatenate([key_rot, value_bf], axis=1), "ctx", axis=0, tiled=True
    )
    key_block = min(1024, seq_len)
    num_blocks = seq_len // key_block
    kv_heads = kv_all.reshape(num_blocks, key_block, 2, KV_HEADS, HEAD_DIM)
    kv_heads = jnp.transpose(kv_heads, (2, 0, 3, 1, 4))
    key_blocks, value_blocks = kv_heads[0], kv_heads[1]
    pos_blocks = all_pos.reshape(num_blocks, key_block)

    def to_groups(rows):
        rows = rows.reshape(row_count, KV_HEADS, group_size, HEAD_DIM)
        return jnp.transpose(rows, (1, 2, 0, 3)).reshape(
            KV_HEADS, group_size * row_count, HEAD_DIM
        )

    def from_groups(rows):
        rows = rows.reshape(KV_HEADS, group_size, row_count, HEAD_DIM)
        return jnp.transpose(rows, (2, 0, 1, 3)).reshape(row_count, q_width)

    def dots(spec, left, right):
        return jnp.einsum(spec, left, right, preferred_element_type=jnp.float32)

    query_group = to_groups(query_rot)
    query_pos = jnp.tile(own_pos, group_size)

    def masked_scores(key_part, pos_part):
        allowed = pos_part[None, :] <= query_pos[:, None]
        scores = dots("gqd,gkd->gqk", query_group, key_part) * scale
        return jnp.where(allowed[None], scores, -jnp.inf)

    exp_sum = sum(
        jnp.sum(jnp.exp(masked_scores(key_blocks[i], pos_blocks[i])), axis=-1, keepdims=True)
        for i in range(num_blocks)
    )
    log_total = jnp.log(exp_sum)
    out_sum = sum(
        dots(
            "gqk,gkd->gqd",
            jnp.exp(masked_scores(key_blocks[i], pos_blocks[i]) - log_total).astype(bf16),
            value_blocks[i],
        )
        for i in range(num_blocks)
    )
    out_group = out_sum.astype(bf16)
    attn_bf = from_groups(out_group)
    middle = token_f32 + dot_plain(attn_bf, out_full)
    rms_mlp, unit_mlp, normed_mlp = norm_forward(middle, gain_mlp)

    normed_all = lax.all_gather(normed_mlp, "ctx", axis=0, tiled=True)
    gate_pre = dot_plain(normed_all, gate_w)
    up_pre = dot_plain(normed_all, up_w)
    sigmoid_gate = jax.nn.sigmoid(gate_pre)
    silu_gate = gate_pre * sigmoid_gate
    hidden = (silu_gate * up_pre).astype(bf16)
    hidden_grad = dot_right_trans(cot_all, down_w)
    gate_back = (
        hidden_grad * up_pre * sigmoid_gate * (1.0 + gate_pre * (1.0 - sigmoid_gate))
    ).astype(bf16)
    up_back = (hidden_grad * silu_gate).astype(bf16)
    normed_mlp_part = dot_right_trans(gate_back, gate_w) + dot_right_trans(up_back, up_w)
    normed_mlp_grad = lax.psum_scatter(
        normed_mlp_part.astype(bf16), "ctx", scatter_dimension=0, tiled=True
    )
    hidden, gate_back, up_back, normed_mlp_grad = lax.optimization_barrier(
        (hidden, gate_back, up_back, normed_mlp_grad)
    )
    normed_mlp_grad = normed_mlp_grad.astype(jnp.float32)

    mlp_back, gain_mlp_part = norm_backward(normed_mlp_grad, rms_mlp, unit_mlp, gain_mlp)
    middle_grad = cot_rows.astype(jnp.float32) + mlp_back
    middle_grad_b = middle_grad.astype(bf16)
    attn_back = dot_right_trans(middle_grad_b, out_full).astype(bf16)
    grad_group = to_groups(attn_back)
    row_delta = jnp.sum(
        grad_group.astype(jnp.float32) * out_group.astype(jnp.float32), axis=-1, keepdims=True
    )
    query_acc = 0.0
    key_pieces, value_pieces = [], []
    for i in range(num_blocks):
        probs_full = jnp.exp(masked_scores(key_blocks[i], pos_blocks[i]) - log_total)
        prob_grad = dots("gqd,gkd->gqk", grad_group, value_blocks[i])
        score_grad = (probs_full * (prob_grad - row_delta) * scale).astype(bf16)
        query_acc = query_acc + dots("gqk,gkd->gqd", score_grad, key_blocks[i])
        key_pieces.append(dots("gqk,gqd->gkd", score_grad, query_group).astype(bf16))
        value_pieces.append(dots("gqk,gqd->gkd", probs_full.astype(bf16), grad_group).astype(bf16))
    kv_pieces = jnp.stack([jnp.stack(key_pieces), jnp.stack(value_pieces)])
    kv_pieces = jnp.transpose(kv_pieces, (1, 3, 0, 2, 4)).reshape(seq_len, 2 * kv_width)
    kv_own = lax.psum_scatter(kv_pieces, "ctx", scatter_dimension=0, tiled=True)

    output_part = dot_plain(hidden, down_w).astype(bf16)
    output_own = lax.psum_scatter(output_part, "ctx", scatter_dimension=0, tiled=True)
    result = (middle + output_own.astype(jnp.float32)).astype(bf16)
    gate_up_part = jnp.concatenate(
        [dot_left_trans(normed_all, gate_back), dot_left_trans(normed_all, up_back)], axis=1
    ).astype(bf16)
    fin_gate_up = scatter_rows(gate_up_part)
    down_part = lax.all_to_all(
        dot_left_trans(hidden, cot_all).astype(bf16),
        "ctx",
        split_axis=1,
        concat_axis=0,
        tiled=True,
    )
    fin_down = scatter_rows(down_part)
    out_mid = lax.psum_scatter(
        dot_left_trans(attn_bf, middle_grad_b).astype(bf16),
        "ctx",
        scatter_dimension=1,
        tiled=True,
    )

    query_back = rotate_back(
        from_groups(query_acc).reshape(row_count, HEADS, HEAD_DIM), cosine, sine
    ).astype(bf16)
    key_back = rotate_back(
        kv_own[:, :kv_width].astype(jnp.float32).reshape(row_count, KV_HEADS, HEAD_DIM),
        cosine,
        sine,
    ).astype(bf16)
    qkv_back = jnp.concatenate(
        [
            query_back.reshape(row_count, ctx_size, q_cols),
            key_back.reshape(row_count, ctx_size, kv_cols),
            kv_own[:, kv_width:].reshape(row_count, ctx_size, kv_cols),
        ],
        axis=2,
    )
    normed_attn_grad = dots("tcf,cdf->td", qkv_back, qkv_full)
    qkv_part = dots("td,tcf->cdf", normed_attn, qkv_back).astype(bf16)
    qkv_mid = lax.psum_scatter(qkv_part, "ctx", scatter_dimension=0, tiled=False)
    fin_attn = scatter_rows(jnp.concatenate([qkv_mid, out_mid], axis=1))
    attn_norm_back, gain_attn_part = norm_backward(normed_attn_grad, rms_attn, unit_attn, gain_attn)
    input_back = (middle_grad + attn_norm_back).astype(bf16)
    gain_attn_sum, gain_mlp_sum = lax.psum((gain_attn_part, gain_mlp_part), ("seq", "fsdp", "ctx"))
    return (
        result.reshape(1, row_count, width),
        input_back.reshape(1, row_count, width),
        gain_attn_sum,
        gain_mlp_sum,
        fin_attn[:, :q_cols],
        fin_attn[:, q_cols : q_cols + kv_cols],
        fin_attn[:, q_cols + kv_cols : qkv_cols],
        fin_attn[:, qkv_cols:attn_cols],
        fin_gate_up[:, :ff_cols],
        fin_gate_up[:, ff_cols:],
        fin_down,
    )


def solution(mesh):
    return jax.shard_map(
        on_device,
        mesh=mesh,
        in_specs=(
            P(("seq", "fsdp"), "ctx", None),
            P(("seq", "fsdp"), "ctx", None),
            P(),
            P(),
            P(),
            P(("seq", "fsdp"), "ctx"),
            P(("seq", "fsdp"), "ctx"),
            P(("seq", "fsdp"), "ctx"),
            P(("seq", "fsdp"), "ctx"),
            P(("seq", "fsdp"), "ctx"),
            P(("seq", "fsdp"), "ctx"),
            P(("seq", "fsdp"), "ctx"),
        ),
        out_specs=(
            P(("seq", "fsdp"), "ctx", None),
            P(("seq", "fsdp"), "ctx", None),
            P(),
            P(),
            P(("seq", "fsdp"), "ctx"),
            P(("seq", "fsdp"), "ctx"),
            P(("seq", "fsdp"), "ctx"),
            P(("seq", "fsdp"), "ctx"),
            P(("seq", "fsdp"), "ctx"),
            P(("seq", "fsdp"), "ctx"),
            P(("seq", "fsdp"), "ctx"),
        ),
        check_vma=False,
    )
```

time: 916 us -> 500 us (0.55)
  waiting for transfers between devices: 622 us -> 264 us
  blocking collectives: 151 us -> 86.3 us
  starting transfers between devices: 1.11 us -> 15.8 us
    reduce_scatter x5 -> x1, waiting for transfers between devices: 237 us -> 0.02 us  [on_device(): lax.psum_scatter(qkv_part, 'ctx', scatter_dimension=0, tiled=False)]
    unnamed x29 -> x15, waiting for transfers between devices: 204 us -> 93.6 us
    all_gather x8 -> x2, blocking collectives: 113 us -> 26.4 us  [the longest x1 14.4 us: on_device(): lax.all_gather(w_down, rows_axes, axis=0, tiled=True)]
    all_gather x8 -> x6, waiting for transfers between devices: 181 us -> 123 us  [the longest x1 39.2 us: on_device(): qkv_full = lax.all_gather(attn_rows[:, :qkv_cols], 'ctx', axis=0)]
    all_to_all x0 -> x4, waiting for transfers between devices: none -> 46.7 us  [the longest x3 27.8 us: scatter_rows(): lax.all_to_all(pieces, rows_axes, split_axis=0, concat_axis=0, tiled=True)]
    all_to_all x0 -> x1, blocking collectives: none -> 21.5 us  [on_device(): lax.all_to_all(lax.all_gather(w_down, rows_axes, axis=0, tiled=True), 'ct...]
    all_to_all x0 -> x4, starting transfers between devices: none -> 15.1 us  [the longest x3 11.4 us: scatter_rows(): lax.all_to_all(pieces, rows_axes, split_axis=0, concat_axis=0, tiled=True)]
    dot_general x14 -> x7, matrix products: 21.7 us -> 24.1 us  [dots(): return jnp.einsum(spec, left, right, preferred_element_type=jnp.float32)]
  transfers between devices with their start and end apart: 21 -> 15, of which waited for: 16 -> 12; matrix products, arithmetic and copies ran while one was open for 9% -> 12% of each run, Pallas kernels for 0% -> 0%
where the time goes in v1:
time: 500 us; the launch traced here: 491 us
  waiting for transfers between devices  264 us (53%)
  blocking collectives  86.3 us (17%)
  matrix products  63.7 us (13%)
  local copies, waits for them, and re-layouts  35.5 us (7%)
  starting transfers between devices  15.8 us (3%)
  between operations  14.8 us (3%)
  other arithmetic  11.2 us (2%)
    unnamed x15, waiting for transfers between devices  93.6 us
    all_gather x1, waiting for transfers between devices, on_device(): qkv_full = lax.all_gather(attn_rows[:, :qkv_cols], 'ctx', axis=0)  39.2 us
    psum x1, blocking collectives, on_device(): lax.psum((gain_attn_part, gain_mlp_part), ('seq', 'fsdp', 'ctx'))  38.4 us
    all_to_all x3, waiting for transfers between devices, scatter_rows(): lax.all_to_all(pieces, rows_axes, split_axis=0, concat_axis=0, tiled=True)  27.8 us
    dot_general x7, matrix products, dots(): return jnp.einsum(spec, left, right, preferred_element_type=jnp.float32)  24.1 us
    all_gather x1, waiting for transfers between devices, on_device(): cot_all = lax.all_gather(cot_rows, 'ctx', axis=0, tiled=True)  23.9 us
    unnamed x73, local copies, waits for them, and re-layouts  23.2 us
    all_gather x1, waiting for transfers between devices, on_device(): lax.all_gather(jnp.concatenate([key_rot, value_bf], axis=1), 'ctx', axis=...  22.2 us
  transfers between devices with their start and end apart: 15, of which 12 were waited for; matrix products, arithmetic and copies ran while one was open for 12% of the time, Pallas kernels for 0%

profile of v1, /device:TPU:0, one launch (start us, length us, event | category | flops | bytes accessed | tf_op | source)
XLA Modules:
  0.0 490.9 jit_solution(13693876611374795985)
XLA Ops:
  9.9 12.0 %all-gather.2 = bf16[4,240,320]{1,2,0:T(8,128)(2,1)S(1)} all-gather(bf16[1,240,320]{1,2,0:T(8,128)(2,1)S(1)} %maximum_bitcast_fusion.1), channel_id=1, replica_groups=mesh['seq'=2,'fsdp'=2,'ctx'=8] {'seq','fsdp'}, dimensions={0}, use_global_device_ids=true | all-gather | bytes 768000 | tf_op jit(solution)/shard_map/all_gather | solution.py:127
  24.4 39.2 %all-gather.21.cloned.1.call-done = bf16[8,960,200]{1,2,0:T(8,128)(2,1)} async-done(((bf16[1,960,200]{1,2,0:T(8,128)(2,1)}), bf16[8,960,200]{1,2,0:T(8,128)(2,1)}) %all-gather.21.cloned.1.call-update) | async-done | bytes 3072016 | tf_op jit(solution)/shard_map/all_gather | solution.py:130
  63.6 3.0 fusion.75
  70.0 22.2 %all-gather.11.cloned.1.call-done = bf16[1024,640]{0,1:T(8,128)(2,1)} async-done(((bf16[128,640]{0,1:T(8,128)(2,1)}), bf16[1024,640]{0,1:T(8,128)(2,1)}) %all-gather.11.cloned.1.call-update) | async-done | bytes 1310736 | tf_op jit(solution)/shard_map/all_gather | solution.py:154
  92.2 8.7 %fusion.1 = f32[5,384,1024]{2,1,0:T(8,128)} fusion(pred[384,1024]{1,0:T(8,128)(4,1)S(1)} %broadcast_compare_fusion, bf16[2,1,5,1024,64]{3,4,2,1,0:T(8,128)(2,1)} %bitcast.157, bf16[128,5,3,32]{0,3,2,1:T(8,128)(2,1)S(1)} %bitcast.180, bf16[128,5,3,32]{0,3,2,1:T(8,128)(2,1)S(1)} %bitcast.178), kind=kOutput, calls=%fused_computation.2 | convolution fusion | flops 514132864 | bytes 10452992 | tf_op jit(solution)/shard_map/reduce_sum | solution.py:186
  100.9 4.7 fusion.27
  105.8 15.8 %all-gather.13.cloned.1.call-done = bf16[960,960]{0,1:T(8,128)(2,1)} async-done(((bf16[960,120]{0,1:T(8,128)(2,1)}), bf16[960,960]{0,1:T(8,128)(2,1)}) %all-gather.13.cloned.1.call-update) | async-done | bytes 1843216 | tf_op jit(solution)/shard_map/all_gather | solution.py:131
  125.6 14.4 %all_gather.35 = bf16[2560,120]{1,0:T(8,128)(2,1)S(1)} all-gather(bf16[640,120]{1,0:T(8,128)(2,1)S(1)} %copy.131), channel_id=1, replica_groups=mesh['seq'=2,'fsdp'=2,'ctx'=8] {'seq','fsdp'}, dimensions={0}, use_global_device_ids=true | all-gather | bytes 768000 | tf_op jit(solution)/shard_map/all_gather | solution.py:137
  139.9 21.5 %all_to_all.50 = bf16[8,320,120]{2,1,0:T(8,128)(2,1)S(1)} all-to-all(bf16[8,320,120]{2,1,0:T(8,128)(2,1)S(1)} %bitcast.164), channel_id=1, replica_groups=mesh['seq'=2,'fsdp'=2,'ctx'=8] {'ctx'}, dimensions={0} | all-to-all | bytes 1228800 | tf_op jit(solution)/shard_map/all_to_all | solution.py:136
  162.4 22.2 %all-gather.15.cloned.1.call-done = bf16[1024,960]{0,1:T(8,128)(2,1)} async-done(((bf16[128,960]{0,1:T(8,128)(2,1)}), bf16[1024,960]{0,1:T(8,128)(2,1)}) %all-gather.15.cloned.1.call-update) | async-done | bytes 1966096 | tf_op jit(solution)/shard_map/all_gather | solution.py:203
  184.6 4.2 fusion.37
  190.8 23.9 %all-gather.19.cloned.1.call-done = bf16[1,1024,960]{1,2,0:T(8,128)(2,1)} async-done(((bf16[1,128,960]{1,2,0:T(8,128)(2,1)}), bf16[1,1024,960]{1,2,0:T(8,128)(2,1)}) %all-gather.19.cloned.1.call-update) | async-done | bytes 1966096 | tf_op jit(solution)/shard_map/all_gather | solution.py:144
  214.7 4.4 multiply_convert_fusion.1
  224.8 35.0 %reduce-scatter.16.cloned.1.call-done = bf16[128,960]{1,0:T(8,128)(2,1)} async-done(((bf16[1024,960]{1,0:T(8,128)(2,1)}), bf16[128,960]{1,0:T(8,128)(2,1)}) %reduce-scatter.16.cloned.1.call-update) | async-done | bytes 245776
  260.9 2.6 convolution_convert_fusion
  266.8 34.2 %reduce-scatter.18.cloned.1.call-done = bf16[128,960]{1,0:T(8,128)(2,1)} async-done(((bf16[1024,960]{1,0:T(8,128)(2,1)}), bf16[128,960]{1,0:T(8,128)(2,1)}) %reduce-scatter.18.cloned.1.call-update) | async-done | bytes 245776
  306.4 4.1 fusion.24
  310.6 4.7 multiply_convert_fusion
  323.3 3.5 fusion.45
  327.2 23.7 %reduce-scatter.20.cloned.1.call-done = bf16[128,640]{1,0:T(8,128)(2,1)} async-done(((bf16[1024,640]{1,0:T(8,128)(2,1)}), bf16[128,640]{1,0:T(8,128)(2,1)}) %reduce-scatter.20.cloned.1.call-update) | async-done | bytes 163856
  352.3 2.8 convert_bitcast_fusion
  360.5 3.8 all-to-all-start.3
  367.1 3.4 convolution_convert_fusion.4
  373.4 18.9 %all-to-all-done.3 = bf16[320,8,120]{2,0,1:T(8,128)(2,1)S(1)} async-done(((bf16[320,8,120]{2,0,1:T(8,128)(2,1)}), bf16[320,8,120]{2,0,1:T(8,128)(2,1)S(1)}, u32[]{:S(2)}, u32[]{:S(2)}) %all-to-all-start.3) | async-done | bytes 614432 | tf_op jit(solution)/shard_map/all_to_all | solution.py:251
  392.3 3.6 all-to-all-start.2
  397.0 13.2 %all-to-all-done.2 = bf16[4,240,640]{2,1,0:T(8,128)(2,1)S(1)} async-done(((bf16[4,240,640]{2,1,0:T(8,128)(2,1)}), bf16[4,240,640]{2,1,0:T(8,128)(2,1)S(1)}, u32[]{:S(2)}, u32[]{:S(2)}) %all-to-all-start.2) | async-done | bytes 1228832 | tf_op jit(solution)/shard_map/all_to_all | solution.py:124
  410.2 3.5 all-to-all-start.4
  415.7 7.1 %all-to-all-done.4 = bf16[4,640,120]{1,2,0:T(8,128)(2,1)S(1)} async-done(((bf16[4,640,120]{1,2,0:T(8,128)(2,1)}), bf16[4,640,120]{1,2,0:T(8,128)(2,1)S(1)}, u32[]{:S(2)}, u32[]{:S(2)}) %all-to-all-start.4) | async-done | bytes 614432 | tf_op jit(solution)/shard_map/all_to_all | solution.py:124
  423.6 3.4 fusion.57
  427.1 38.4 %all-reduce = (f32[960]{0:T(1024)}, f32[960]{0:T(1024)}) all-reduce(f32[960]{0:T(1024)S(1)} %get-tuple-element.98, f32[960]{0:T(1024)S(1)} %get-tuple-element.96), channel_id=1, replica_groups=mesh['seq'=2,'fsdp'=2,'ctx'=8] {'seq','fsdp','ctx'}, use_global_device_ids=true, to_apply=%region_11.12 | all-reduce | flops 1920 | bytes 15360 | tf_op jit(solution)/shard_map/psum | solution.py:288
  469.2 4.2 all-to-all-start.1
  474.4 7.5 %all-to-all-done.1 = bf16[4,240,320]{1,2,0:T(8,128)(2,1)S(1)} async-done(((bf16[4,240,320]{1,2,0:T(8,128)(2,1)}), bf16[4,240,320]{1,2,0:T(8,128)(2,1)S(1)}, u32[]{:S(2)}, u32[]{:S(2)}) %all-to-all-start.1) | async-done | bytes 614432 | tf_op jit(solution)/shard_map/all_to_all | solution.py:124
  (168 shorter events, 62.1 us)
Async XLA Ops:
  7.2 56.4 %all-gather.21.cloned.1.call-start = ((), (), s32[]{:S(2)}) async-start(), calls=%async_computation.16 | async-start | bytes 3686400 | tf_op jit(solution)/shard_map/all_gather | solution.py:130
  21.9 2.2 copy-start.2
  21.9 41.6 %copy-start.23 = (f32[960]{0:T(1024)S(1)}, f32[960]{0:T(1024)}, u32[]{:S(2)}) copy-start(f32[960]{0:T(1024)} %param.15) | copy-start | bytes 11524
  23.8 68.4 %all-gather.11.cloned.1.call-start = ((), (), s32[]{:S(2)}) async-start(), calls=%async_computation.10 | async-start | bytes 1474560 | tf_op jit(solution)/shard_map/all_gather | solution.py:154
  67.4 54.1 %all-gather.13.cloned.1.call-start = ((), (), s32[]{:S(2)}) async-start(), calls=%async_computation.11 | async-start | bytes 2211840 | tf_op jit(solution)/shard_map/all_gather | solution.py:131
  68.2 94.2 %all-gather.17.cloned.1.call-start = ((), (), s32[]{:S(2)}) async-start(), calls=%async_computation.13 | async-start | bytes 1536000 | tf_op jit(solution)/shard_map/all_gather | solution.py:132
  69.5 115.1 %all-gather.15.cloned.1.call-start = ((), (), s32[]{:S(2)}) async-start(), calls=%async_computation.12 | async-start | bytes 2211840 | tf_op jit(solution)/shard_map/all_gather | solution.py:203
  70.0 31.0 %copy-start.15 = (bf16[128,15,32]{0,2,1:T(8,128)(2,1)}, bf16[128,15,32]{0,2,1:T(8,128)(2,1)S(1)}, u32[]{:S(2)}) copy-start(bf16[128,15,32]{0,2,1:T(8,128)(2,1)S(1)} %get-tuple-element.111) | copy-start | bytes 368644
  70.0 31.0 %copy-start.17 = (bf16[128,15,32]{0,2,1:T(8,128)(2,1)}, bf16[128,15,32]{0,2,1:T(8,128)(2,1)S(1)}, u32[]{:S(2)}) copy-start(bf16[128,15,32]{0,2,1:T(8,128)(2,1)S(1)} %get-tuple-element.112) | copy-start | bytes 368644
  92.2 8.7 %copy-start.5 = (bf16[1024,640]{0,1:T(8,128)(2,1)S(1)}, bf16[1024,640]{0,1:T(8,128)(2,1)}, u32[]{:S(2)}) copy-start(bf16[1024,640]{0,1:T(8,128)(2,1)} %all-gather.11.cloned.1.call-done) | copy-start | bytes 3932164
  105.6 18.2 %copy-start.22 = (f32[960]{0:T(1024)S(1)}, f32[960]{0:T(1024)}, u32[]{:S(2)}) copy-start(f32[960]{0:T(1024)} %param.16) | copy-start | bytes 11524
  105.8 19.0 %copy-start.9 = (bf16[128,5,3,64]{0,3,2,1:T(8,128)(2,1)}, bf16[128,5,3,64]{0,3,2,1:T(8,128)(2,1)S(1)}, u32[]{:S(2)}) copy-start(bf16[128,5,3,64]{0,3,2,1:T(8,128)(2,1)S(1)} %copy.128) | copy-start | bytes 737284
  121.5 3.9 copy-start.21
  124.8 89.9 %all-gather.19.cloned.1.call-start = ((), (), s32[]{:S(2)}) async-start(), calls=%async_computation.15 | async-start | bytes 2211840 | tf_op jit(solution)/shard_map/all_gather | solution.py:144
  125.4 134.4 %reduce-scatter.16.cloned.1.call-start = ((), (), s32[]{:S(2)}) async-start(), calls=%async_computation.17 | async-start | bytes 2359296
  162.4 52.3 %copy-start.13 = (bf16[320,960]{1,0:T(8,128)(2,1)}, bf16[320,960]{1,0:T(8,128)(2,1)S(1)}, u32[]{:S(2)}) copy-start(bf16[320,960]{1,0:T(8,128)(2,1)S(1)} %all_to_all.38) | copy-start | bytes 1843204
  162.4 26.4 %copy-start.3 = (bf16[960,640]{1,0:T(8,128)(2,1)S(1)}, bf16[960,640]{1,0:T(8,128)(2,1)}, u32[]{:S(2)}) copy-start(bf16[960,640]{1,0:T(8,128)(2,1)} %all-gather.17.cloned.1.call-done) | copy-start | bytes 3686404
  184.6 4.2 copy-start.25
  224.8 76.2 %reduce-scatter.18.cloned.1.call-start = ((), (), s32[]{:S(2)}) async-start(), calls=%async_computation.18 | async-start | bytes 2359296
  260.9 5.5 %copy-start.8 = (bf16[128,960]{0,1:T(8,128)(2,1)}, bf16[128,960]{0,1:T(8,128)(2,1)S(1)}, u32[]{:S(2)}) copy-start(bf16[128,960]{0,1:T(8,128)(2,1)S(1)} %copy.151) | copy-start | bytes 737284
  266.1 38.7 %copy-start.1 = (bf16[960,960]{0,1:T(8,128)(2,1)S(1)}, bf16[960,960]{0,1:T(8,128)(2,1)}, u32[]{:S(2)}) copy-start(bf16[960,960]{0,1:T(8,128)(2,1)} %all-gather.13.cloned.1.call-done) | copy-start | bytes 5529604
  266.2 84.7 %reduce-scatter.20.cloned.1.call-start = ((), (), s32[]{:S(2)}) async-start(), calls=%async_computation.19 | async-start | bytes 1474560
  306.4 4.2 copy-start.6
  310.5 4.7 copy-start.16
  310.5 4.7 copy-start.18
  318.8 146.7 %reduce-scatter.22.cloned.1.call-start = ((), (), s32[]{:S(2)}) async-start(), calls=%async_computation.20 | async-start | bytes 2211840
  322.0 144.8 %reduce-scatter.14.cloned.1.call-start = ((), (), s32[]{:S(2)}) async-start(), calls=%async_computation.14 | async-start | bytes 3686400 | tf_op jit(solution)/shard_map/reduce_scatter | solution.py:284
  358.7 5.5 %copy-start.12 = (bf16[1024,320]{0,1:T(8,128)(2,1)S(1)}, bf16[1024,320]{0,1:T(8,128)(2,1)}, u32[]{:S(2)}) copy-start(bf16[1024,320]{0,1:T(8,128)(2,1)} %copy-done.11) | copy-start | bytes 1966084
  360.5 31.8 %all-to-all-start.3 = ((bf16[320,8,120]{2,0,1:T(8,128)(2,1)}), bf16[320,8,120]{2,0,1:T(8,128)(2,1)S(1)}, u32[]{:S(2)}, u32[]{:S(2)}) async-start(bf16[320,8,120]{2,0,1:T(8,128)(2,1)} %copy.140), calls=%async_computation.4 | async-start | bytes 1310720 | tf_op jit(solution)/shard_map/all_to_all | solution.py:251
  392.3 17.9 %all-to-all-start.2 = ((bf16[4,240,640]{2,1,0:T(8,128)(2,1)}), bf16[4,240,640]{2,1,0:T(8,128)(2,1)S(1)}, u32[]{:S(2)}, u32[]{:S(2)}) async-start(bf16[4,240,640]{2,1,0:T(8,128)(2,1)} %pad_maximum_fusion.1), calls=%async_computation.3 | async-start | bytes 2457600 | tf_op jit(solution)/shard_map/all_to_all | solution.py:124
  410.2 12.7 %all-to-all-start.4 = ((bf16[4,640,120]{1,2,0:T(8,128)(2,1)}), bf16[4,640,120]{1,2,0:T(8,128)(2,1)S(1)}, u32[]{:S(2)}, u32[]{:S(2)}) async-start(bf16[4,640,120]{1,2,0:T(8,128)(2,1)} %copy.141), calls=%async_computation.5 | async-start | bytes 1228800 | tf_op jit(solution)/shard_map/all_to_all | solution.py:124
  469.2 12.7 %all-to-all-start.1 = ((bf16[4,240,320]{1,2,0:T(8,128)(2,1)}), bf16[4,240,320]{1,2,0:T(8,128)(2,1)S(1)}, u32[]{:S(2)}, u32[]{:S(2)}) async-start(bf16[4,240,320]{1,2,0:T(8,128)(2,1)} %pad_maximum_fusion.2), calls=%async_computation.2 | async-start | bytes 1310720 | tf_op jit(solution)/shard_map/all_to_all | solution.py:124
  (10 other events, 15.4 us)
Sparse Core Ops, SparseCore 0:
  23.9 39.5 all-gather.20
  67.6 24.5 all-gather.10
  94.4 27.0 all-gather.12
  123.8 29.0 all-gather.16
  154.9 29.6 all-gather.14
  186.0 28.6 all-gather.18
  224.9 34.8 reduce-scatter.15
  266.3 34.6 reduce-scatter.17
  318.9 31.9 reduce-scatter.19
  353.1 40.1 reduce-scatter.21
  395.6 43.3 reduce-scatter.13

commit v2 on v1

--- a/solution.py
+++ b/solution.py
@@ -127,24 +127,23 @@
     attn_rows = lax.all_gather(
         jnp.concatenate([w_query, w_key, w_value, w_out], axis=1), rows_axes, axis=0, tiled=True
     )
-    qkv_full = lax.all_gather(attn_rows[:, :qkv_cols], "ctx", axis=0)
-    out_full = lax.all_gather(attn_rows[:, qkv_cols:], "ctx", axis=1, tiled=True)
-    gate_up = lax.all_gather(
-        jnp.concatenate([w_gate, w_up], axis=1), rows_axes, axis=0, tiled=True
-    )
-    gate_w, up_w = gate_up[:, :ff_cols], gate_up[:, ff_cols:]
-    down_w = lax.all_to_all(
-        lax.all_gather(w_down, rows_axes, axis=0, tiled=True),
-        "ctx",
-        split_axis=0,
-        concat_axis=1,
-        tiled=True,
-    )
     cot_rows = cotangent[0]
     cot_all = lax.all_gather(cot_rows, "ctx", axis=0, tiled=True)
-
+    attn_rows, cot_all = lax.optimization_barrier((attn_rows, cot_all))
+    attn_full = lax.all_gather(attn_rows, "ctx", axis=0)
+    qkv_full = attn_full[:, :, :qkv_cols]
+    out_full = jnp.transpose(attn_full[:, :, qkv_cols:], (1, 0, 2)).reshape(q_width, width)
+    down_rows = lax.all_gather(w_down, rows_axes, axis=0, tiled=True)
+    down_w = lax.all_to_all(down_rows, "ctx", split_axis=0, concat_axis=1, tiled=True)
+    gate_in, _ = lax.optimization_barrier((w_gate, down_w))
+    gate_w = lax.all_gather(gate_in, rows_axes, axis=0, tiled=True)
+    up_in, _ = lax.optimization_barrier((w_up, gate_w))
+    up_w = lax.all_gather(up_in, rows_axes, axis=0, tiled=True)
     token_f32 = tokens[0].astype(jnp.float32)
     rms_attn, unit_attn, normed_attn = norm_forward(token_f32, gain_attn)
+    normed_attn, gate_w, up_w, down_w = lax.optimization_barrier(
+        (normed_attn, gate_w, up_w, down_w)
+    )
     qkv = jnp.einsum("td,cdf->tcf", normed_attn, qkv_full, preferred_element_type=jnp.float32)
     query_raw = qkv[:, :, :q_cols].reshape(row_count, HEADS, HEAD_DIM)
     key_raw = qkv[:, :, q_cols : q_cols + kv_cols].reshape(row_count, KV_HEADS, HEAD_DIM)
@@ -239,11 +238,11 @@
         value_pieces.append(dots("gqk,gqd->gkd", probs_full.astype(bf16), grad_group).astype(bf16))
     kv_pieces = jnp.stack([jnp.stack(key_pieces), jnp.stack(value_pieces)])
     kv_pieces = jnp.transpose(kv_pieces, (1, 3, 0, 2, 4)).reshape(seq_len, 2 * kv_width)
+    kv_pieces, hidden, gate_back, up_back, middle_late = lax.optimization_barrier(
+        (kv_pieces, hidden, gate_back, up_back, middle_grad_b)
+    )
     kv_own = lax.psum_scatter(kv_pieces, "ctx", scatter_dimension=0, tiled=True)
 
-    output_part = dot_plain(hidden, down_w).astype(bf16)
-    output_own = lax.psum_scatter(output_part, "ctx", scatter_dimension=0, tiled=True)
-    result = (middle + output_own.astype(jnp.float32)).astype(bf16)
     gate_up_part = jnp.concatenate(
         [dot_left_trans(normed_all, gate_back), dot_left_trans(normed_all, up_back)], axis=1
     ).astype(bf16)
@@ -256,12 +255,11 @@
         tiled=True,
     )
     fin_down = scatter_rows(down_part)
-    out_mid = lax.psum_scatter(
-        dot_left_trans(attn_bf, middle_grad_b).astype(bf16),
-        "ctx",
-        scatter_dimension=1,
-        tiled=True,
-    )
+    out_part = dots(
+        "td,tcf->cdf", attn_bf, middle_late.reshape(row_count, ctx_size, width // ctx_size)
+    ).astype(bf16)
+    out_pieces = lax.all_to_all(out_part, "ctx", split_axis=0, concat_axis=0, tiled=True)
+    out_mid = jnp.sum(out_pieces.astype(jnp.float32), axis=0).astype(bf16)
 
     query_back = rotate_back(
         from_groups(query_acc).reshape(row_count, HEADS, HEAD_DIM), cosine, sine
@@ -282,10 +280,18 @@
     normed_attn_grad = dots("tcf,cdf->td", qkv_back, qkv_full)
     qkv_part = dots("td,tcf->cdf", normed_attn, qkv_back).astype(bf16)
     qkv_mid = lax.psum_scatter(qkv_part, "ctx", scatter_dimension=0, tiled=False)
+    output_part, qkv_mid = lax.optimization_barrier(
+        (dot_plain(hidden, down_w).astype(bf16), qkv_mid)
+    )
+    output_own = lax.psum_scatter(output_part, "ctx", scatter_dimension=0, tiled=True)
+    result = (middle + output_own.astype(jnp.float32)).astype(bf16)
     fin_attn = scatter_rows(jnp.concatenate([qkv_mid, out_mid], axis=1))
     attn_norm_back, gain_attn_part = norm_backward(normed_attn_grad, rms_attn, unit_attn, gain_attn)
     input_back = (middle_grad + attn_norm_back).astype(bf16)
-    gain_attn_sum, gain_mlp_sum = lax.psum((gain_attn_part, gain_mlp_part), ("seq", "fsdp", "ctx"))
+    gain_parts = lax.all_gather(
+        jnp.stack([gain_attn_part, gain_mlp_part]), ("seq", "fsdp", "ctx"), axis=0
+    )
+    gain_attn_sum, gain_mlp_sum = jnp.sum(gain_parts, axis=0)
     return (
         result.reshape(1, row_count, width),
         input_back.reshape(1, row_count, width),

time: 500 us -> 504 us (level)
  waiting for transfers between devices: 264 us -> 245 us
  local copies, waits for them, and re-layouts: 35.5 us -> 49.9 us
  starting transfers between devices: 15.8 us -> 23.3 us
    all_to_all x0 -> x2, waiting for transfers between devices: none -> 78.3 us  [the longest x1 44.2 us: on_device(): lax.all_to_all(out_part, 'ctx', split_axis=0, concat_axis=0, tiled=True)]
    all_gather x1 -> x4, blocking collectives: 14.4 us -> 74.7 us  [the longest x1 40.9 us: on_device(): lax.all_gather(jnp.stack([gain_attn_part, gain_mlp_part]), ('seq', 'fsdp'...]
    all_gather x3 -> x1, waiting for transfers between devices: 55 us -> 0.01 us  [on_device(): attn_full = lax.all_gather(attn_rows, 'ctx', axis=0)]
    psum x1 -> x0, blocking collectives: 38.4 us -> none  [on_device(): lax.psum((gain_attn_part, gain_mlp_part), ('seq', 'fsdp', 'ctx'))]
    unnamed x15 -> x11, waiting for transfers between devices: 93.6 us -> 63.8 us
    all_to_all x1 -> x0, blocking collectives: 21.5 us -> none  [on_device(): lax.all_to_all(lax.all_gather(w_down, rows_axes, axis=0, tiled=True), 'ct...]
    all_to_all x3, waiting for transfers between devices: 27.8 us -> 20.4 us  [scatter_rows(): lax.all_to_all(pieces, rows_axes, split_axis=0, concat_axis=0, tiled=True)]
    all_to_all x0 -> x2, starting transfers between devices: none -> 7.37 us  [the longest x1 3.77 us: on_device(): lax.all_to_all(down_rows, 'ctx', split_axis=0, concat_axis=1, tiled=True)]
  transfers between devices with their start and end apart: 15 -> 14, of which waited for: 12 -> 10; matrix products, arithmetic and copies ran while one was open for 12% -> 13% of each run, Pallas kernels for 0% -> 0%
where the time goes in v2:
time: 504 us; the launch traced here: 498 us
  waiting for transfers between devices  245 us (49%)
  blocking collectives  86.8 us (17%)
  matrix products  61.6 us (12%)
  local copies, waits for them, and re-layouts  49.9 us (10%)
  starting transfers between devices  23.3 us (5%)
  other arithmetic  16 us (3%)
  between operations  15.4 us (3%)
    unnamed x11, waiting for transfers between devices  63.8 us
    all_to_all x1, waiting for transfers between devices, on_device(): lax.all_to_all(out_part, 'ctx', split_axis=0, concat_axis=0, tiled=True)  44.2 us
    all_gather x1, blocking collectives, on_device(): lax.all_gather(jnp.stack([gain_attn_part, gain_mlp_part]), ('seq', 'fsdp'...  40.9 us
    all_to_all x1, waiting for transfers between devices, on_device(): lax.all_to_all(down_rows, 'ctx', split_axis=0, concat_axis=1, tiled=True)  34.1 us
    all_gather x1, waiting for transfers between devices, on_device(): normed_all = lax.all_gather(normed_mlp, 'ctx', axis=0, tiled=True)  28.8 us
    dot_general x8, matrix products, dots(): return jnp.einsum(spec, left, right, preferred_element_type=jnp.float32)  27.5 us
    unnamed x103, local copies, waits for them, and re-layouts  22.4 us
    all_to_all x3, waiting for transfers between devices, scatter_rows(): lax.all_to_all(pieces, rows_axes, split_axis=0, concat_axis=0, tiled=True)  20.4 us
  transfers between devices with their start and end apart: 14, of which 10 were waited for; matrix products, arithmetic and copies ran while one was open for 13% of the time, Pallas kernels for 0%

profile of v2, /device:TPU:0, one launch (start us, length us, event | category | flops | bytes accessed | tf_op | source)
XLA Modules:
  0.0 497.7 jit_solution(11553839972049547633)
XLA Ops:
  10.6 12.2 %all-gather.5 = bf16[4,240,320]{1,2,0:T(8,128)(2,1)S(1)} all-gather(bf16[1,240,320]{1,2,0:T(8,128)(2,1)S(1)} %maximum_bitcast_fusion.1), channel_id=1, replica_groups=mesh['seq'=2,'fsdp'=2,'ctx'=8] {'seq','fsdp'}, dimensions={0}, use_global_device_ids=true | all-gather | bytes 768000 | tf_op jit(solution)/shard_map/all_gather | solution.py:127
  24.7 17.2 %all-gather.17.cloned.1.call-done = bf16[1,1024,960]{1,2,0:T(8,128)(2,1)} async-done(((bf16[1,128,960]{1,2,0:T(8,128)(2,1)}), bf16[1,1024,960]{1,2,0:T(8,128)(2,1)}) %all-gather.17.cloned.1.call-update) | async-done | bytes 1966096 | tf_op jit(solution)/shard_map/all_gather | solution.py:131
  42.2 12.2 %all_gather.33 = bf16[2560,120]{1,0:T(8,128)(2,1)} all-gather(bf16[640,120]{1,0:T(8,128)(2,1)S(1)} %copy.122), channel_id=1, replica_groups=mesh['seq'=2,'fsdp'=2,'ctx'=8] {'seq','fsdp'}, dimensions={0}, use_global_device_ids=true | all-gather | bytes 768000 | tf_op jit(solution)/shard_map/all_gather | solution.py:136
  54.4 3.8 all-to-all-start
  60.2 34.1 %all-to-all-done = bf16[8,320,120]{2,1,0:T(8,128)(2,1)S(1)} async-done(((bf16[8,320,120]{2,1,0:T(8,128)(2,1)}), bf16[8,320,120]{2,1,0:T(8,128)(2,1)S(1)}, u32[]{:S(2)}, u32[]{:S(2)}) %all-to-all-start) | async-done | bytes 614432 | tf_op jit(solution)/shard_map/all_to_all | solution.py:137
  96.0 10.3 %all-gather.3 = bf16[4,240,320]{1,2,0:T(8,128)(2,1)S(1)} all-gather(bf16[1,240,320]{1,2,0:T(8,128)(2,1)S(1)} %bitcast.207), channel_id=1, replica_groups=mesh['seq'=2,'fsdp'=2,'ctx'=8] {'seq','fsdp'}, dimensions={0}, use_global_device_ids=true | all-gather | bytes 768000 | tf_op jit(solution)/shard_map/all_gather | solution.py:139
  108.2 11.2 %all-gather.4 = bf16[4,240,320]{1,2,0:T(8,128)(2,1)S(1)} all-gather(bf16[1,240,320]{1,2,0:T(8,128)(2,1)S(1)} %bitcast.208), channel_id=1, replica_groups=mesh['seq'=2,'fsdp'=2,'ctx'=8] {'seq','fsdp'}, dimensions={0}, use_global_device_ids=true | all-gather | bytes 768000 | tf_op jit(solution)/shard_map/all_gather | solution.py:141
  132.2 18.3 %all-gather.13.cloned.1.call-done = bf16[1024,640]{0,1:T(8,128)(2,1)} async-done(((bf16[128,640]{0,1:T(8,128)(2,1)}), bf16[1024,640]{0,1:T(8,128)(2,1)}) %all-gather.13.cloned.1.call-update) | async-done | bytes 1310736 | tf_op jit(solution)/shard_map/all_gather | solution.py:153
  150.5 9.2 %fusion.1 = f32[5,384,1024]{2,1,0:T(8,128)} fusion(pred[384,1024]{1,0:T(8,128)(4,1)} %broadcast_compare_fusion, bf16[2,1,5,1024,64]{3,4,2,1,0:T(8,128)(2,1)} %bitcast.175, bf16[128,5,3,32]{0,3,2,1:T(8,128)(2,1)} %bitcast.197, bf16[128,5,3,32]{0,3,2,1:T(8,128)(2,1)} %bitcast.195), kind=kOutput, calls=%fused_computation.2 | convolution fusion | flops 514132864 | bytes 10452992 | tf_op jit(solution)/shard_map/reduce_sum | solution.py:185
  159.6 5.3 %fusion.20 = bf16[5,384,64]{1,2,0:T(8,128)(2,1)} fusion(f32[5,384,1024]{2,1,0:T(8,128)} %fusion.1, bf16[2,1,5,1024,64]{3,4,2,1,0:T(8,128)(2,1)S(1)} %bitcast.177), kind=kOutput, calls=%fused_computation.37 | convolution fusion | flops 253747200 | bytes 8765440 | tf_op jit(solution)/shard_map/gqk,gkd->gqd/dot_general | solution.py:174
  168.4 28.8 %all-gather.15.cloned.1.call-done = bf16[1024,960]{0,1:T(8,128)(2,1)} async-done(((bf16[128,960]{0,1:T(8,128)(2,1)}), bf16[1024,960]{0,1:T(8,128)(2,1)}) %all-gather.15.cloned.1.call-update) | async-done | bytes 1966096 | tf_op jit(solution)/shard_map/all_gather | solution.py:202
  207.5 3.9 copy.147
  211.7 35.0 %reduce-scatter.13.cloned.1.call-done = bf16[128,960]{1,0:T(8,128)(2,1)} async-done(((bf16[1024,960]{1,0:T(8,128)(2,1)}), bf16[128,960]{1,0:T(8,128)(2,1)}) %reduce-scatter.13.cloned.1.call-update) | async-done | bytes 245776
  250.5 4.2 fusion.17
  254.7 4.7 multiply_convert_fusion
  262.9 3.6 fusion.31
  266.9 28.0 %reduce-scatter.15.cloned.1.call-done = bf16[128,640]{1,0:T(8,128)(2,1)} async-done(((bf16[1024,640]{1,0:T(8,128)(2,1)}), bf16[128,640]{1,0:T(8,128)(2,1)}) %reduce-scatter.15.cloned.1.call-update) | async-done | bytes 163856
  304.3 4.2 all-to-all-start.4
  308.5 3.5 convolution_convert_fusion.3
  313.5 3.3 convolution_convert_fusion.4
  319.7 17.8 %all-to-all-done.4 = bf16[320,8,120]{2,0,1:T(8,128)(2,1)} async-done(((bf16[320,8,120]{2,0,1:T(8,128)(2,1)}), bf16[320,8,120]{2,0,1:T(8,128)(2,1)}, u32[]{:S(2)}, u32[]{:S(2)}) %all-to-all-start.4) | async-done | bytes 614432 | tf_op jit(solution)/shard_map/all_to_all | solution.py:250
  337.5 3.7 all-to-all-start.3
  343.4 13.3 %all-to-all-done.3 = bf16[4,240,640]{2,1,0:T(8,128)(2,1)S(1)} async-done(((bf16[4,240,640]{2,1,0:T(8,128)(2,1)}), bf16[4,240,640]{2,1,0:T(8,128)(2,1)S(1)}, u32[]{:S(2)}, u32[]{:S(2)}) %all-to-all-start.3) | async-done | bytes 1228832 | tf_op jit(solution)/shard_map/all_to_all | solution.py:124
  356.7 3.7 all-to-all-start.5
  362.5 7.1 %all-to-all-done.5 = bf16[4,640,120]{1,2,0:T(8,128)(2,1)S(1)} async-done(((bf16[4,640,120]{1,2,0:T(8,128)(2,1)}), bf16[4,640,120]{1,2,0:T(8,128)(2,1)S(1)}, u32[]{:S(2)}, u32[]{:S(2)}) %all-to-all-start.5) | async-done | bytes 614432 | tf_op jit(solution)/shard_map/all_to_all | solution.py:124
  370.5 3.6 all-to-all-start.1
  374.1 3.8 convolution_convert_fusion
  377.9 3.9 copy.151
  389.0 4.3 fusion.43
  393.3 44.2 %all-to-all-done.1 = bf16[8,960,120]{1,2,0:T(8,128)(2,1)S(1)} async-done(((bf16[8,960,120]{1,2,0:T(8,128)(2,1)}), bf16[8,960,120]{1,2,0:T(8,128)(2,1)S(1)}, u32[]{:S(2)}, u32[]{:S(2)}) %all-to-all-start.1) | async-done | bytes 1843232 | tf_op jit(solution)/shard_map/all_to_all | solution.py:261
  440.5 3.6 all-to-all-start.2
  444.2 40.9 %all-gather.7 = f32[32,2,960]{2,1,0:T(2,128)S(1)} all-gather(f32[1,2,960]{2,1,0:T(2,128)S(1)} %maximum_bitcast_fusion.2), channel_id=4, replica_groups=mesh['seq'=2,'fsdp'=2,'ctx'=8] {'seq','fsdp','ctx'}, dimensions={0}, use_global_device_ids=true | all-gather | bytes 253440 | tf_op jit(solution)/shard_map/all_gather | solution.py:291
  (204 shorter events, 79.6 us)
Async XLA Ops:
  7.2 34.8 %all-gather.17.cloned.1.call-start = ((), (), s32[]{:S(2)}) async-start(), calls=%async_computation.13 | async-start | bytes 2211840 | tf_op jit(solution)/shard_map/all_gather | solution.py:131
  7.9 113.5 %all-gather.19.cloned.1.call-start = ((), (), s32[]{:S(2)}) async-start(), calls=%async_computation.14 | async-start | bytes 5898240 | tf_op jit(solution)/shard_map/all_gather | solution.py:133
  10.6 31.4 %copy-start.28 = (bf16[640,120]{0,1:T(8,128)(2,1)S(1)}, bf16[640,120]{0,1:T(8,128)(2,1)}, u32[]{:S(2)}) copy-start(bf16[640,120]{0,1:T(8,128)(2,1)} %param.23) | copy-start | bytes 460804
  23.3 34.9 %copy-start.41 = (s32[16]{0:T(128)S(1)}, s32[16]{0:T(128)}, u32[]{:S(2)}) copy-start(s32[16]{0:T(128)} %param.14) | copy-start | bytes 196
  23.3 35.7 %copy-start.3 = (bf16[1,128,960]{1,2,0:T(8,128)(2,1)S(1)}, bf16[1,128,960]{1,2,0:T(8,128)(2,1)}, u32[]{:S(2)}) copy-start(bf16[1,128,960]{1,2,0:T(8,128)(2,1)} %param.12) | copy-start | bytes 737284
  24.7 34.5 %copy-start.32 = (f32[960]{0:T(1024)S(1)}, f32[960]{0:T(1024)}, u32[]{:S(2)}) copy-start(f32[960]{0:T(1024)} %param.15) | copy-start | bytes 11524
  54.4 39.8 %all-to-all-start = ((bf16[8,320,120]{2,1,0:T(8,128)(2,1)}), bf16[8,320,120]{2,1,0:T(8,128)(2,1)S(1)}, u32[]{:S(2)}, u32[]{:S(2)}) async-start(bf16[8,320,120]{2,1,0:T(8,128)(2,1)} %bitcast.3), calls=%async_computation | async-start | bytes 1310720 | tf_op jit(solution)/shard_map/all_to_all | solution.py:137
  58.2 37.9 %copy-start.26 = (bf16[240,320]{0,1:T(8,128)(2,1)S(1)}, bf16[240,320]{0,1:T(8,128)(2,1)}, u32[]{:S(2)}) copy-start(bf16[240,320]{0,1:T(8,128)(2,1)} %param.21) | copy-start | bytes 460804
  58.2 92.3 %all-gather.13.cloned.1.call-start = ((), (), s32[]{:S(2)}) async-start(), calls=%async_computation.10 | async-start | bytes 1474560 | tf_op jit(solution)/shard_map/all_gather | solution.py:153
  58.3 35.9 %copy-start.31 = (s32[1024]{0:T(1024)}, s32[1024]{0:T(1024)S(1)}, u32[]{:S(2)}) copy-start(s32[1024]{0:T(1024)S(1)} %fusion.64) | copy-start | bytes 12292
  59.1 35.1 %copy-start.37 = (f32[128]{0:T(128)}, f32[128]{0:T(128)S(1)}, u32[]{:S(2)}) copy-start(f32[128]{0:T(128)S(1)} %add_rsqrt_fusion.1) | copy-start | bytes 1540
  126.0 71.1 %all-gather.15.cloned.1.call-start = ((), (), s32[]{:S(2)}) async-start(), calls=%async_computation.11 | async-start | bytes 2211840 | tf_op jit(solution)/shard_map/all_gather | solution.py:202
  166.7 30.5 %copy-start.6 = (bf16[960,320]{0,1:T(8,128)(2,1)S(1)}, bf16[960,320]{0,1:T(8,128)(2,1)}, u32[]{:S(2)}) copy-start(bf16[960,320]{0,1:T(8,128)(2,1)} %reshape.274) | copy-start | bytes 1843204
  167.4 81.4 %copy-start.35 = (f32[128]{0:T(128)}, f32[128]{0:T(128)S(1)}, u32[]{:S(2)}) copy-start(f32[128]{0:T(128)S(1)} %add_rsqrt_fusion) | copy-start | bytes 1540
  168.3 78.4 %reduce-scatter.13.cloned.1.call-start = ((), (), s32[]{:S(2)}) async-start(), calls=%async_computation.15 | async-start | bytes 2359296
  211.4 37.4 %copy-start.12 = (bf16[1,128,960]{1,2,0:T(8,128)(2,1)S(1)}, bf16[1,128,960]{1,2,0:T(8,128)(2,1)}, u32[]{:S(2)}) copy-start(bf16[1,128,960]{1,2,0:T(8,128)(2,1)} %param.13) | copy-start | bytes 737284
  211.4 83.5 %reduce-scatter.15.cloned.1.call-start = ((), (), s32[]{:S(2)}) async-start(), calls=%async_computation.16 | async-start | bytes 1474560
  262.9 115.0 %reduce-scatter.11.cloned.1.call-start = ((), (), s32[]{:S(2)}) async-start(), calls=%async_computation.12 | async-start | bytes 3686400 | tf_op jit(solution)/shard_map/reduce_scatter | solution.py:282
  266.7 29.6 %copy-start.15 = (bf16[128,960]{0,1:T(8,128)(2,1)S(1)}, bf16[128,960]{0,1:T(8,128)(2,1)}, u32[]{:S(2)}) copy-start(bf16[128,960]{0,1:T(8,128)(2,1)} %fusion.37) | copy-start | bytes 737284
  266.9 32.2 %copy-start.18 = (bf16[128,15,64]{0,2,1:T(8,128)(2,1)}, bf16[128,15,64]{0,2,1:T(8,128)(2,1)S(1)}, u32[]{:S(2)}) copy-start(bf16[128,15,64]{0,2,1:T(8,128)(2,1)S(1)} %pad_maximum_fusion.4) | copy-start | bytes 737284
  304.3 33.2 %all-to-all-start.4 = ((bf16[320,8,120]{2,0,1:T(8,128)(2,1)}), bf16[320,8,120]{2,0,1:T(8,128)(2,1)}, u32[]{:S(2)}, u32[]{:S(2)}) async-start(bf16[320,8,120]{2,0,1:T(8,128)(2,1)} %copy.137), calls=%async_computation.5 | async-start | bytes 1310720 | tf_op jit(solution)/shard_map/all_to_all | solution.py:250
  319.7 40.8 %copy-start.10 = (bf16[128,5,3,64]{0,3,2,1:T(8,128)(2,1)S(1)}, bf16[128,5,3,64]{0,3,2,1:T(8,128)(2,1)}, u32[]{:S(2)}) copy-start(bf16[128,5,3,64]{0,3,2,1:T(8,128)(2,1)} %copy-done.9) | copy-start | bytes 737284
  337.5 19.2 %all-to-all-start.3 = ((bf16[4,240,640]{2,1,0:T(8,128)(2,1)}), bf16[4,240,640]{2,1,0:T(8,128)(2,1)S(1)}, u32[]{:S(2)}, u32[]{:S(2)}) async-start(bf16[4,240,640]{2,1,0:T(8,128)(2,1)} %pad_maximum_fusion.1), calls=%async_computation.4 | async-start | bytes 2457600 | tf_op jit(solution)/shard_map/all_to_all | solution.py:124
  356.7 12.8 %all-to-all-start.5 = ((bf16[4,640,120]{1,2,0:T(8,128)(2,1)}), bf16[4,640,120]{1,2,0:T(8,128)(2,1)S(1)}, u32[]{:S(2)}, u32[]{:S(2)}) async-start(bf16[4,640,120]{1,2,0:T(8,128)(2,1)} %copy.138), calls=%async_computation.6 | async-start | bytes 1228800 | tf_op jit(solution)/shard_map/all_to_all | solution.py:124
  370.5 67.1 %all-to-all-start.1 = ((bf16[8,960,120]{1,2,0:T(8,128)(2,1)}), bf16[8,960,120]{1,2,0:T(8,128)(2,1)S(1)}, u32[]{:S(2)}, u32[]{:S(2)}) async-start(bf16[8,960,120]{1,2,0:T(8,128)(2,1)} %convert_bitcast_fusion.1), calls=%async_computation.2 | async-start | bytes 3932160 | tf_op jit(solution)/shard_map/all_to_all | solution.py:261
  374.1 114.0 %reduce-scatter.17.cloned.1.call-start = ((), (), s32[]{:S(2)}) async-start(), calls=%async_computation.17 | async-start | bytes 2359296
  440.5 48.7 %copy-start.13 = (bf16[1,128,960]{1,2,0:T(8,128)(2,1)S(1)}, bf16[1,128,960]{1,2,0:T(8,128)(2,1)}, u32[]{:S(2)}) copy-start(bf16[1,128,960]{1,2,0:T(8,128)(2,1)} %param.13) | copy-start | bytes 737284
  440.5 48.7 %copy-start.21 = (f32[128,960]{0,1:T(8,128)S(1)}, f32[128,960]{0,1:T(8,128)}, u32[]{:S(2)}) copy-start(f32[128,960]{0,1:T(8,128)} %get-tuple-element.159) | copy-start | bytes 1474564
  440.5 48.7 %copy-start.30 = (f32[960]{0:T(1024)S(1)}, f32[960]{0:T(1024)}, u32[]{:S(2)}) copy-start(f32[960]{0:T(1024)} %param.16) | copy-start | bytes 11524
  440.5 48.7 %copy-start.36 = (f32[128]{0:T(128)S(1)}, f32[128]{0:T(128)}, u32[]{:S(2)}) copy-start(f32[128]{0:T(128)} %copy-done.35) | copy-start | bytes 1540
  440.5 48.7 %copy-start.40 = (f32[128]{0:T(128)S(1)}, f32[128]{0:T(128)}, u32[]{:S(2)}) copy-start(f32[128]{0:T(128)} %copy-done.39) | copy-start | bytes 1540
  440.5 45.2 %all-to-all-start.2 = ((bf16[4,240,320]{1,2,0:T(8,128)(2,1)}), bf16[4,240,320]{1,2,0:T(8,128)(2,1)S(1)}, u32[]{:S(2)}, u32[]{:S(2)}) async-start(bf16[4,240,320]{1,2,0:T(8,128)(2,1)} %copy.133), calls=%async_computation.3 | async-start | bytes 1310720 | tf_op jit(solution)/shard_map/all_to_all | solution.py:124
  (28 other events, 101.7 us)
Sparse Core Ops, SparseCore 0:
  9.6 32.3 all-gather.16
  43.6 68.8 all-gather.18
  126.1 24.3 all-gather.12
  168.4 28.6 all-gather.14
  211.6 35.0 reduce-scatter.12
  263.0 31.8 reduce-scatter.14
  299.2 49.8 reduce-scatter.10
  381.9 56.4 reduce-scatter.16
